TPU v7x, 512 devices: a whole 4x4x16 slice. The times are simulated.
512 devices in a mesh: rep: 64 (over z, y), row: 8 (over x, core).
Axes of the slice: x: 4, y: 4, z: 16, core: 2. Of those that a mesh axis runs over, the one named last changes fastest.
Arguments:
- momentum: float32 [64, 8192, 128], P('rep', 'row'), may hold values from -6 to 6
- inputs: bfloat16 [64, 1024, 8192], P('rep', None, 'row'), may hold values from -6 to 6
- out_grads: bfloat16 [64, 1024, 128], P('rep', 'row'), may hold values from -0.19921875 to 0.19921875
- chosen: int32 [64, 64, 1, 8], P('rep', 'row'), may hold values from 0 to 128, as said below
Outputs:
- new_momentum: float32 [64, 8192, 128], P('rep', 'row')
- update: float32 [8192, 128], P('row')
Inputs may be any that keep to these rules, and one draw needn't show every extreme that they name: `chosen`: for each replica and block, the first c entries, with 1 <= c <= 8, are distinct coefficient rows below 128, and the remaining entries equal 128; on every device the first block has 8 entries.
All inputs are finite; a program needn't handle non-finite values.
Results may differ from a plain program's by a relative error of at most 0.0003.
Values may be sent and summed in bfloat16 or wider, within the bound.
No kernel may reach another device: no remote copies, remote signals or barrier semaphores. Data moves between devices by JAX's collectives and lax.ppermute only.
A program may use at most 64 MiB of HBM per device.

v0:
```python
import jax
import jax.numpy as jnp
from jax import lax
from jax.sharding import PartitionSpec as P

CH = 128
K = 8


PRECISE = lax.Precision.HIGHEST
MOMENTUM_DECAY = 0.999


def basis_table(order):
    frequency = jnp.arange(order, dtype=jnp.float32)[:, None]
    sample = jnp.arange(order, dtype=jnp.float32)[None, :]
    norm_scale = jnp.where(frequency == 0.0, jnp.sqrt(1.0 / order), jnp.sqrt(2.0 / order))
    return norm_scale * jnp.cos(jnp.pi * (2.0 * sample + 1.0) * frequency / (2.0 * order))


def to_blocks(matrix):
    row_total, col_total = matrix.shape
    return matrix.reshape(row_total // CH, CH, col_total // CH, CH).transpose(0, 2, 1, 3)


def from_blocks(blocks):
    row_blocks, col_blocks = (blocks.shape[0], blocks.shape[1])
    return blocks.transpose(0, 2, 1, 3).reshape(row_blocks * CH, col_blocks * CH)


def forward(blocks, basis):
    left = jnp.einsum("kn,abnm->abkm", basis, blocks, precision=PRECISE)
    return jnp.einsum("abkm,jm->abkj", left, basis, precision=PRECISE)


def inverse(coeffs, basis):
    left = jnp.einsum("kn,abkj->abnj", basis, coeffs, precision=PRECISE)
    return jnp.einsum("abnj,jm->abnm", left, basis, precision=PRECISE)


def body(momentum, inputs, out_grads, chosen):
    moment_old = momentum[0]
    activations = inputs[0]
    basis = basis_table(CH)
    weight_grad = lax.dot_general(
        activations,
        lax.all_gather(out_grads[0], "row", axis=0, tiled=True),
        (((0,), (0,)), ((), ())),
        preferred_element_type=jnp.float32,
    )
    moment = MOMENTUM_DECAY * moment_old + weight_grad
    coeffs = forward(to_blocks(moment), basis)
    chosen_rows = chosen[0]
    one_hot = (chosen_rows[..., None] == jnp.arange(CH, dtype=jnp.int32)).astype(jnp.float32)
    selected = jnp.einsum("abqk,abkj->abqj", one_hot, coeffs, precision=PRECISE)
    placed = jnp.einsum("abqk,abqj->abkj", one_hot, selected, precision=PRECISE)
    moment_new = moment - from_blocks(inverse(placed, basis))
    row_blocks, col_blocks = (placed.shape[0], placed.shape[1])
    block_count = row_blocks * col_blocks
    flat_selected = selected.reshape(block_count, K, CH)
    flat_rows = chosen_rows.reshape(block_count, K).astype(jnp.float32)
    values = lax.all_gather(flat_selected, "rep", axis=1, tiled=True)
    positions = lax.all_gather(flat_rows, "rep", axis=1, tiled=True)
    row_hot = (positions[..., None] == jnp.arange(CH, dtype=jnp.float32)).astype(jnp.float32)
    summed = jnp.einsum("cqk,cqj->ckj", row_hot, values, precision=PRECISE)
    update = from_blocks(inverse(summed.reshape(row_blocks, col_blocks, CH, CH), basis))
    return (moment_new[None], update)


def solution(mesh):
    in_specs = (
        P("rep", "row", None),
        P("rep", None, "row"),
        P("rep", "row", None),
        P("rep", "row", None, None),
    )
    out_specs = (P("rep", "row", None), P("row", None))
    return jax.shard_map(body, mesh=mesh, in_specs=in_specs, out_specs=out_specs, check_vma=False)
```

profile of v0, /device:TPU:14, one launch (start us, length us, event | category | flops | bytes accessed | tf_op | source)
XLA Modules:
  0.0 178.7 jit_solution(16161453960248593057)
XLA Ops:
  7.2 0.0 copy-start
  7.2 0.0 all-gather.3.cloned.1.call-start
  7.2 13.2 %all-gather = bf16[1,1024,128]{2,1,0:T(8,128)(2,1)S(1)} all-gather(bf16[1,128,128]{2,1,0:T(8,128)(2,1)} %param.6), channel_id=2, replica_groups=mesh['rep'=64,'row'=8] {'row'}, dimensions={1}, use_global_device_ids=true | all-gather | bytes 294912 | tf_op jit(solution)/shard_map/all_gather | solution.py:47
  20.4 0.0 copy-done
  20.4 1.8 fusion.3
  22.2 0.0 copy-start.1
  22.2 1.1 convolution_bitcast_fusion
  23.4 1.2 fusion.13
  24.5 0.0 copy-done.1
  24.5 1.0 fusion.36
  25.5 0.0 all-gather.3.cloned.1.call-update
  25.6 0.1 copy.10
  25.6 88.6 %all_gather.10 = f32[8,512]{0,1:T(8,128)S(1)} all-gather(f32[8,8]{0,1:T(8,128)S(1)} %copy.10), channel_id=1, replica_groups=mesh['rep'=64,'row'=8] {'rep'}, dimensions={1}, use_global_device_ids=true | all-gather | bytes 16640 | tf_op jit(solution)/shard_map/all_gather | solution.py:63
  114.2 0.1 copy.11
  114.3 1.4 fusion.35
  115.8 0.9 fusion.11
  116.7 1.7 fusion.6
  118.4 47.0 %all-gather.3.cloned.1.call-done = f32[8,512,128]{2,1,0:T(8,128)} async-done(((f32[8,8,128]{2,1,0:T(8,128)}), f32[8,512,128]{2,1,0:T(8,128)}) %all-gather.3.cloned.1.call-update) | async-done | bytes 2097168 | tf_op jit(solution)/shard_map/all_gather | solution.py:62
  165.4 3.9 %fusion.2 = f32[8,128,128]{2,1,0:T(8,128)S(1)} fusion(f32[8,512,128]{2,1,0:T(8,128)} %all-gather.3.cloned.1.call-done, f32[8,512]{1,0:T(8,128)S(1)} %copy.11), kind=kOutput, calls=%fused_computation.3 | convolution fusion | flops 805830656 | bytes 2637824 | tf_op jit(solution)/shard_map/cqk,cqj->ckj/dot_general | solution.py:65
  169.3 0.9 fusion.9
  170.2 1.7 fusion.16
  (2 shorter events, 0.0 us)
Async XLA Ops:
  7.2 13.3 %copy-start = (bf16[1,1024,1024]{2,1,0:T(8,128)(2,1)S(1)}, bf16[1,1024,1024]{2,1,0:T(8,128)(2,1)}, u32[]{:S(2)}) copy-start(bf16[1,1024,1024]{2,1,0:T(8,128)(2,1)} %param.5) | copy-start | bytes 6291460
  7.2 158.2 %all-gather.3.cloned.1.call-start = ((), (), s32[]{:S(2)}) async-start(), calls=%async_computation | async-start | bytes 2129920 | tf_op jit(solution)/shard_map/all_gather | solution.py:62
  22.2 2.3 %copy-start.1 = (s32[1,8,1,8]{3,2,1,0:T(1,128)S(1)}, s32[1,8,1,8]{3,2,1,0:T(1,128)}, u32[]{:S(2)}) copy-start(s32[1,8,1,8]{3,2,1,0:T(1,128)} %param.7) | copy-start | bytes 772
Sparse Core Ops, SparseCore 0:
  25.7 139.6 all-gather.2
where the time goes:
time: 179 us
  blocking collectives  102 us (57%)
  waiting for transfers between devices  47 us (26%)
  matrix products  15.6 us (9%)
  between operations  14.1 us (8%)
    all_gather x1, blocking collectives, body(): positions = lax.all_gather(flat_rows, 'rep', axis=1, tiled=True)  88.6 us
    all_gather x1, waiting for transfers between devices, body(): values = lax.all_gather(flat_selected, 'rep', axis=1, tiled=True)  47 us
    all_gather x1, blocking collectives, body(): lax.all_gather(out_grads[0], 'row', axis=0, tiled=True)  13.2 us
    dot_general x1, matrix products, body(): summed = jnp.einsum('cqk,cqj->ckj', row_hot, values, precision=PRECISE)  3.94 us
  transfers between devices with their start and end apart: 1, of which 1 were waited for; matrix products, arithmetic and copies ran while one was open for 2% of the time, Pallas kernels for 0%

commit v1 on v0

v1 whole, which is shorter than its diff:
```python
import jax
import jax.numpy as jnp
import numpy as np
from jax import lax
from jax.experimental import pallas as pl
from jax.experimental.pallas import tpu as pltpu
from jax.sharding import PartitionSpec as P

CH = 128
K = 8
BLOCKS = 8
GROUPS = 8
WIDTH = CH // GROUPS
REPS = 64
NZ, NY = 16, 4
MOMENTUM_DECAY = 0.999
HIGHEST = lax.Precision.HIGHEST

Z_GROUPS = [[z * NY + y for z in range(NZ)] for y in range(NY)]
Y_GROUPS = [[z * NY + y for y in range(NY)] for z in range(NZ)]


def basis_rows():
    frequency = np.arange(CH, dtype=np.float64)[:, None]
    sample = np.arange(CH, dtype=np.float64)[None, :]
    scale = np.where(frequency == 0.0, np.sqrt(1.0 / CH), np.sqrt(2.0 / CH))
    basis = scale * np.cos(np.pi * (2.0 * sample + 1.0) * frequency / (2.0 * CH))
    return np.concatenate([basis, np.zeros((8, CH))]).astype(np.float32)


def dot(a, b, dims):
    return lax.dot_general(a, b, (dims, ((), ())), precision=HIGHEST, preferred_element_type=jnp.float32)


def project(chosen_s, chosen_v, basis, momentum, inputs, grads, new_momentum, message, picked, partial):
    for i in range(BLOCKS * K):
        row = chosen_s[i // K, i % K]
        picked[i : i + 1, :] = basis[pl.ds(row, 1), :]
    grad = lax.dot_general(
        inputs[...], grads[...], (((0,), (0,)), ((), ())), preferred_element_type=jnp.float32
    )
    for b in range(BLOCKS):
        rows = slice(b * CH, (b + 1) * CH)
        moment = MOMENTUM_DECAY * momentum[rows, :] + grad[rows, :]
        own = picked[b * K : (b + 1) * K, :]
        left = dot(own, moment, ((1,), (0,)))
        partial[b * K : (b + 1) * K, :] = left
        new_momentum[rows, :] = moment - dot(own, left, ((0,), (0,)))
    slot = lax.broadcasted_iota(jnp.int32, (BLOCKS, CH), 1) // WIDTH
    places = jnp.zeros((BLOCKS, CH), jnp.float32)
    per_slot = []
    for q in range(K):
        places = jnp.where(slot == q, chosen_v[:, q : q + 1].astype(jnp.float32), places)
        per_slot.append(partial[pl.ds(q, BLOCKS, stride=K), :])
    for g in range(GROUPS):
        row = jnp.zeros((BLOCKS, CH), jnp.float32)
        for q in range(K):
            turn = ((q - g) * WIDTH) % CH
            moved = per_slot[q] if turn == 0 else pltpu.roll(per_slot[q], turn, 1)
            row = jnp.where(slot == q, moved, row)
        message[g * BLOCKS : (g + 1) * BLOCKS, 0, :] = row
        message[g * BLOCKS : (g + 1) * BLOCKS, 1, :] = places


def combine(basis, received, piece):
    values = received[:, 0, :].T
    places = received[:, 1, :].astype(jnp.int32)
    rows = lax.broadcasted_iota(jnp.int32, (REPS, CH), 1)
    total = jnp.zeros((WIDTH, CH), jnp.float32)
    for q in range(K):
        hot = (places[:, q * WIDTH : q * WIDTH + 1] == rows).astype(jnp.float32)
        total = total + dot(values[q * WIDTH : (q + 1) * WIDTH, :], hot, ((1,), (0,)))
    done = dot(total, basis[:CH, :], ((1,), (0,)))
    for z in range(NZ):
        piece[z, :, :] = done


def place(gathered, update):
    for b in range(BLOCKS):
        parts = [gathered[b % NY, 2 * g + b // NY, :, :] for g in range(GROUPS)]
        update[b * CH : (b + 1) * CH, :] = jnp.concatenate(parts, axis=0).T


def in_vmem(n):
    return [pl.BlockSpec(memory_space=pltpu.VMEM)] * n


def body(momentum, inputs, out_grads, chosen):
    table = jnp.asarray(basis_rows())
    picks = chosen.reshape(BLOCKS, K)
    grads = lax.all_to_all(
        jnp.broadcast_to(out_grads, (8,) + out_grads.shape[1:]), "row", 0, 0, tiled=True
    )
    new_momentum, message = pl.pallas_call(
        project,
        name="project",
        out_shape=(
            jax.ShapeDtypeStruct((BLOCKS * CH, CH), jnp.float32),
            jax.ShapeDtypeStruct((REPS, 2, CH), jnp.float32),
        ),
        in_specs=[pl.BlockSpec(memory_space=pltpu.SMEM)] + in_vmem(5),
        out_specs=tuple(in_vmem(2)),
        scratch_shapes=[
            pltpu.VMEM((BLOCKS * K, CH), jnp.float32),
            pltpu.VMEM((BLOCKS * K, CH), jnp.float32),
        ],
    )(picks, picks, table, momentum[0], inputs[0], grads.reshape(-1, CH))
    received = lax.all_to_all(message, "rep", 0, 0, tiled=True)
    piece = pl.pallas_call(
        combine,
        name="combine",
        out_shape=jax.ShapeDtypeStruct((NZ, WIDTH, CH), jnp.float32),
        in_specs=in_vmem(2),
        out_specs=in_vmem(1)[0],
    )(table, received)
    along_z = lax.all_to_all(piece, "rep", 0, 0, axis_index_groups=Z_GROUPS, tiled=True)
    along_y = lax.all_to_all(
        jnp.broadcast_to(along_z, (NY,) + along_z.shape), "rep", 0, 0, axis_index_groups=Y_GROUPS, tiled=True
    )
    update = pl.pallas_call(
        place,
        name="place",
        out_shape=jax.ShapeDtypeStruct((BLOCKS * CH, CH), jnp.float32),
        in_specs=in_vmem(1),
        out_specs=in_vmem(1)[0],
    )(along_y)
    return new_momentum[None], update


def solution(mesh):
    in_specs = (
        P("rep", "row", None),
        P("rep", None, "row"),
        P("rep", "row", None),
        P("rep", "row", None, None),
    )
    out_specs = (P("rep", "row", None), P("row", None))
    return jax.shard_map(body, mesh=mesh, in_specs=in_specs, out_specs=out_specs, check_vma=False)
```

time: 179 us -> 84.6 us (0.47)
  the two profiles are of different devices: /device:TPU:14 before, /device:TPU:32 now
where the time goes in v1:
time: 84.6 us; the launch traced here: 84.1 us
  blocking collectives  72.8 us (86%)
  Pallas kernels  9.75 us (12%)
    all_to_all x1, blocking collectives, body(): received = lax.all_to_all(message, 'rep', 0, 0, tiled=True)  32.9 us
    all_to_all x1, blocking collectives, body(): lax.all_to_all(piece, 'rep', 0, 0, axis_index_groups=Z_GROUPS, tiled=True)  17.1 us
    all_to_all x1, blocking collectives, body(): lax.all_to_all(jnp.broadcast_to(out_grads, (8,) + out_grads.shape[1:]), '...  11.7 us
    all_to_all x1, blocking collectives, body(): lax.all_to_all(jnp.broadcast_to(along_z, (NY,) + along_z.shape), 'rep', 0...  11.2 us
    pallas_call x1, Pallas kernels, body(): pl.pallas_call(project, name='project', out_shape=(jax.ShapeDtypeStruct((...  5.14 us
    pallas_call x1, Pallas kernels, body(): pl.pallas_call(combine, name='combine', out_shape=jax.ShapeDtypeStruct((N...  2.57 us
    pallas_call x1, Pallas kernels, body(): pl.pallas_call(place, name='place', out_shape=jax.ShapeDtypeStruct((BLOCK...  2.04 us

profile of v1, /device:TPU:32, one launch (start us, length us, event | category | flops | bytes accessed | tf_op | source)
XLA Modules:
  0.0 84.1 jit_solution(11781040686302128171)
XLA Ops:
  0.6 0.8 broadcast_in_dim.14
  1.4 11.7 %all_to_all.20 = bf16[8,128,128]{2,1,0:T(8,128)(2,1)} all-to-all(bf16[8,128,128]{2,1,0:T(8,128)(2,1)S(1)} %broadcast_in_dim.14), channel_id=1, replica_groups=mesh['rep'=64,'row'=8] {'row'}, dimensions={0} | all-to-all | bytes 524288 | tf_op jit(solution)/shard_map/all_to_all | solution.py:91
  13.1 5.1 %project.1 = (f32[1024,128]{1,0:T(8,128)}, f32[64,2,128]{2,1,0:T(2,128)}) custom-call(s32[8,8]{1,0:T(8,128)} %bitcast.10, s32[8,8]{1,0:T(8,128)} %bitcast.11, f32[136,128]{1,0:T(8,128)} %constant.2.clone.basis, f32[1024,128]{1,0:T(8,128)} %bitcast.8, bf16[1024,1024]{1,0:T(8,128)(2,1)} %bitcast.6, bf16[1024,128]{1,0:T(8,128)(2,1)} %bitcast.7), custom_call_target="tpu_custom_call" | custom-call | tf_op jit(solution)/shard_map/project/pallas_call | solution.py:94
  18.3 32.9 %all_to_all.21.received = f32[64,2,128]{2,1,0:T(2,128)} all-to-all(f32[64,2,128]{2,1,0:T(2,128)} %get-tuple-element.5), channel_id=1, replica_groups=mesh['rep'=64,'row'=8] {'rep'}, dimensions={0} | all-to-all | bytes 131072 | tf_op jit(solution)/shard_map/all_to_all | solution.py:108
  51.2 2.6 %combine.1 = f32[16,16,128]{2,1,0:T(8,128)} custom-call(f32[136,128]{1,0:T(8,128)} %constant.2.clone.basis, f32[64,2,128]{2,1,0:T(2,128)} %all_to_all.21.received), custom_call_target="tpu_custom_call" | custom-call | tf_op jit(solution)/shard_map/combine/pallas_call | solution.py:109
  53.8 17.1 %all_to_all.22 = f32[16,16,128]{2,1,0:T(8,128)S(1)} all-to-all(f32[16,16,128]{2,1,0:T(8,128)} %combine.1), channel_id=1, replica_groups={{0,32,64,96,128,160,192,224,256,288,320,352,384,416,448,480},{8,40,72,1..., dimensions={0} | all-to-all | bytes 262144 | tf_op jit(solution)/shard_map/all_to_all | solution.py:116
  70.9 11.2 %all_to_all.23.gathered = f32[4,16,16,128]{3,2,1,0:T(8,128)} all-to-all(f32[4,16,16,128]{3,2,1,0:T(8,128)S(1)} %broadcast_in_dim.16), channel_id=1, replica_groups={{0,8,16,24},{32,40,48,56},{64,72,80,88},{96,104,112,120},{128,136,144,1..., dimensions={0} | all-to-all | bytes 1048576 | tf_op jit(solution)/shard_map/all_to_all | solution.py:117
  82.0 2.0 %place.1 = f32[1024,128]{1,0:T(8,128)} custom-call(f32[4,16,16,128]{3,2,1,0:T(8,128)} %all_to_all.23.gathered), custom_call_target="tpu_custom_call" | custom-call | tf_op jit(solution)/shard_map/place/pallas_call | solution.py:120
  (1 shorter events, 0.0 us)

commit v2 on v0

v2 whole, which is shorter than its diff:
```python
import jax
import jax.numpy as jnp
import numpy as np
from jax import lax
from jax.experimental import pallas as pl
from jax.experimental.pallas import tpu as pltpu
from jax.sharding import PartitionSpec as P

CH = 128
K = 8
BLOCKS = 8
PICKS = BLOCKS * K
ROWS = 8
TOK = 1024
NZ, NY = 16, 4
MOMENTUM_DECAY = 0.999
BITS = 15
TOP = 32767.0
HIGHEST = lax.Precision.HIGHEST
F32, BF16, I32, I16 = jnp.float32, jnp.bfloat16, jnp.int32, jnp.int16

Z_GROUPS = [[z * NY + y for z in range(NZ)] for y in range(NY)]
Y_GROUPS = [[z * NY + y for y in range(NY)] for z in range(NZ)]


def basis_rows():
    frequency = np.arange(CH, dtype=np.float64)[:, None]
    sample = np.arange(CH, dtype=np.float64)[None, :]
    scale = np.where(frequency == 0.0, np.sqrt(1.0 / CH), np.sqrt(2.0 / CH))
    basis = scale * np.cos(np.pi * (2.0 * sample + 1.0) * frequency / (2.0 * CH))
    return np.concatenate([basis, np.zeros((8, CH))]).astype(np.float32)


def dot(a, b, dims, precision=None):
    return lax.dot_general(a, b, (dims, ((), ())), precision=precision, preferred_element_type=F32)


def halves(a):
    high = a.astype(BF16)
    return high, (a - high.astype(F32)).astype(BF16)


def block(b):
    return slice(b * CH, (b + 1) * CH)


def picks(b):
    return slice(b * K, (b + 1) * K)


def exponent(values, axis):
    most = jnp.max(jnp.abs(values), axis=axis, keepdims=True)
    return jnp.ceil(jnp.log2(jnp.maximum(most, 1e-30)) + 0.01)


def encode(values, power):
    scaled = jnp.round(values * jnp.exp2(BITS - power))
    return jnp.clip(scaled, -TOP, TOP).astype(I32)


def prepare(chosen, basis, momentum, inputs, picked, base, weights, places):
    slot = lax.broadcasted_iota(I32, (K, CH), 0)
    lane = lax.broadcasted_iota(I32, (K, CH), 1)
    numbers = jnp.zeros((K, CH), I32)
    for i in range(PICKS):
        b, q = i // K, i % K
        row = chosen[b, q]
        picked[i : i + 1, :] = basis[pl.ds(row, 1), :]
        numbers = jnp.where((slot == q) & (lane == b), row, numbers)
    places[...] = numbers
    for b in range(BLOCKS):
        own = picked[picks(b), :]
        base[picks(b), :] = dot(own, MOMENTUM_DECAY * momentum[block(b), :], ((1,), (0,)), HIGHEST)
        both = jnp.concatenate(halves(own), axis=0)
        product = dot(both, inputs[:, block(b)], ((1,), (1,)))
        high, low = halves(product[:K] + product[K:])
        weights[picks(b), :] = high
        weights[PICKS + b * K : PICKS + (b + 1) * K, :] = low


def pack(base, weights, places, grads, message, left):
    product = dot(weights[...], grads[...], ((1,), (0,)))
    own = base[...] + product[:PICKS] + product[PICKS:]
    left[...] = own
    power = exponent(own, 1)
    codes = encode(own, power).astype(I16)
    lane = lax.broadcasted_iota(I32, (K, CH), 1)
    notes = places[...]
    for b in range(BLOCKS):
        notes = jnp.where(lane == BLOCKS + b, power[picks(b), :].astype(I32), notes)
    notes = notes.astype(I16)
    for z in range(NZ):
        message[z, :PICKS, :] = codes
        message[z, PICKS:, :] = notes


def subtract(picked, left, momentum, inputs, grads, new_momentum, done):
    grad = dot(inputs[...], grads[...], ((0,), (0,)))
    for b in range(BLOCKS):
        sent = dot(picked[picks(b), :], left[picks(b), :], ((0,), (0,)), HIGHEST)
        new_momentum[block(b), :] = MOMENTUM_DECAY * momentum[block(b), :] + grad[block(b), :] - sent
    done[...] = picked[:8, :]


def combine(basis, received, after, message):
    del after
    notes = received[:, PICKS:, :].astype(I32).reshape(NZ * K, CH)
    scales = jnp.exp2(notes.astype(F32) - BITS)
    rows = lax.broadcasted_iota(I32, (NZ * K, CH), 1)
    powers = []
    for b in range(BLOCKS):
        codes = received[:, picks(b), :].astype(I32).reshape(NZ * K, CH)
        high = lax.shift_right_arithmetic(codes, 8)
        low = codes - high * 256
        terms = jnp.concatenate([high.astype(F32).astype(BF16), low.astype(F32).astype(BF16)], axis=1)
        hot = jnp.where(notes[:, b : b + 1] == rows, scales[:, BLOCKS + b : BLOCKS + b + 1], 0.0).astype(BF16)
        sums = dot(hot, terms, ((0,), (0,)))
        own = dot(basis[:CH, :], 256.0 * sums[:, :CH] + sums[:, CH:], ((0,), (0,)), HIGHEST)
        power = exponent(own, 0)
        powers.append(power)
        coded = encode(own, power).astype(I16)
        for y in range(NY):
            message[y, block(b), :] = coded
    powers = jnp.concatenate(powers, axis=0).astype(I32).astype(I16)
    for y in range(NY):
        message[y, BLOCKS * CH :, :] = powers


def finish(received, update):
    for b in range(BLOCKS):
        total = jnp.zeros((CH, CH), F32)
        for y in range(NY):
            power = received[y, BLOCKS * CH :, :].astype(I32)[b : b + 1, :].astype(F32)
            total = total + received[y, block(b), :].astype(I32).astype(F32) * jnp.exp2(power - BITS)
        update[block(b), :] = total


def call(kernel, out, operands, spaces=None, flops=0, limit=4, scratch=()):
    spaces = spaces or [pltpu.VMEM] * len(operands)
    moved = sum(a.size * a.dtype.itemsize for a in operands) + sum(o.size * o.dtype.itemsize for o in out)
    return pl.pallas_call(
        kernel,
        name=kernel.__name__,
        out_shape=tuple(out),
        in_specs=[pl.BlockSpec(memory_space=s) for s in spaces],
        out_specs=tuple(pl.BlockSpec(memory_space=pltpu.VMEM) for _ in out),
        scratch_shapes=list(scratch),
        compiler_params=pltpu.CompilerParams(vmem_limit_bytes=int(limit * 2**20)),
        cost_estimate=pl.CostEstimate(flops=flops, bytes_accessed=moved, transcendentals=0),
    )(*operands)


def array(shape, dtype=F32):
    return jax.ShapeDtypeStruct(shape, dtype)


def body(momentum, inputs, out_grads, chosen):
    momentum, inputs = momentum[0], inputs[0]
    table = jnp.asarray(basis_rows())
    copies = jnp.broadcast_to(out_grads, (ROWS,) + out_grads.shape[1:])
    grads = lax.all_to_all(copies, "row", 0, 0, tiled=True).reshape(TOK, CH)
    picked, base, weights, places = call(
        prepare,
        [array((PICKS, CH)), array((PICKS, CH)), array((2 * PICKS, TOK), BF16), array((K, CH), I32)],
        [chosen.reshape(BLOCKS, K), table, momentum, inputs],
        spaces=[pltpu.SMEM, pltpu.VMEM, pltpu.VMEM, pltpu.VMEM],
        flops=2 * 2 * PICKS * CH * TOK,
    )
    message, left = call(
        pack,
        [array((NZ, PICKS + K, CH), I16), array((PICKS, CH))],
        [base, weights, places, grads],
        flops=2 * 2 * PICKS * CH * TOK,
    )
    along_z = lax.all_to_all(message, "rep", 0, 0, axis_index_groups=Z_GROUPS, tiled=True)
    new_momentum, after = call(
        subtract,
        [array((BLOCKS * CH, CH)), array((8, CH))],
        [picked, left, momentum, inputs, grads],
        flops=2 * BLOCKS * CH * CH * TOK,
    )
    (message,) = call(
        combine,
        [array((NY, BLOCKS * CH + BLOCKS, CH), I16)],
        [table, along_z, after],
        limit=8,
    )
    along_y = lax.all_to_all(message, "rep", 0, 0, axis_index_groups=Y_GROUPS, tiled=True)
    (update,) = call(finish, [array((BLOCKS * CH, CH))], [along_y])
    return new_momentum[None], update


def solution(mesh):
    in_specs = (
        P("rep", "row", None),
        P("rep", None, "row"),
        P("rep", "row", None),
        P("rep", "row", None, None),
    )
    out_specs = (P("rep", "row", None), P("row", None))
    return jax.shard_map(body, mesh=mesh, in_specs=in_specs, out_specs=out_specs, check_vma=False)
```

time: 179 us -> 70.2 us (0.39)
  the two profiles are of different devices: /device:TPU:14 before, /device:TPU:32 now
where the time goes in v2:
time: 70.2 us; the launch traced here: 69.8 us
  starting transfers between devices  19.5 us (28%)
  waiting for transfers between devices  19.2 us (27%)
  blocking collectives  18.2 us (26%)
  Pallas kernels  7.42 us (11%)
  local copies, waits for them, and re-layouts  4.72 us (7%)
    all_to_all x1, blocking collectives, body(): lax.all_to_all(message, 'rep', 0, 0, axis_index_groups=Y_GROUPS, tiled=True)  18.2 us
    all_to_all x1, waiting for transfers between devices, body(): lax.all_to_all(message, 'rep', 0, 0, axis_index_groups=Z_GROUPS, tiled=True)  16.6 us
    all_to_all x1, starting transfers between devices, body(): lax.all_to_all(message, 'rep', 0, 0, axis_index_groups=Z_GROUPS, tiled=True)  15.2 us
    pallas_call x5, Pallas kernels, call(): pl.pallas_call(kernel, name=kernel.__name__, out_shape=tuple(out), in_spe...  7.42 us
    all_to_all x1, starting transfers between devices, body(): grads = lax.all_to_all(copies, 'row', 0, 0, tiled=True).reshape(TOK, CH)  4.3 us
    unnamed x12, local copies, waits for them, and re-layouts  3.17 us
    all_to_all x1, waiting for transfers between devices, body(): grads = lax.all_to_all(copies, 'row', 0, 0, tiled=True).reshape(TOK, CH)  2.63 us
    broadcast_in_dim x1, local copies, waits for them, and re-layouts, body(): copies = jnp.broadcast_to(out_grads, (ROWS,) + out_grads.shape[1:])  1.55 us
  transfers between devices with their start and end apart: 2, of which 2 were waited for; matrix products, arithmetic and copies ran while one was open for 0% of the time, Pallas kernels for 5%

profile of v2, /device:TPU:32, one launch (start us, length us, event | category | flops | bytes accessed | tf_op | source)
XLA Modules:
  0.0 69.8 jit_solution(2138668131879356136)
XLA Ops:
  0.6 0.0 copy-start.2
  0.6 1.6 %broadcast_in_dim.11 = bf16[8,128,128]{2,1,0:T(8,128)(2,1)} broadcast(bf16[128,128]{1,0:T(8,128)(2,1)} %bitcast.13), dimensions={1,2} | broadcast | bytes 294912 | tf_op jit(solution)/shard_map/broadcast_in_dim | solution.py:160
  2.2 4.3 %all-to-all-start = ((bf16[8,128,128]{2,1,0:T(8,128)(2,1)}), bf16[8,128,128]{2,1,0:T(8,128)(2,1)S(1)}, u32[]{:S(2)}, u32[]{:S(2)}) async-start(bf16[8,128,128]{2,1,0:T(8,128)(2,1)} %broadcast_in_dim.11), calls=%async_computation | async-start | bytes 524288 | tf_op jit(solution)/shard_map/all_to_all | solution.py:161
  6.5 0.0 copy-done.2
  6.5 0.0 copy-start
  6.5 1.6 %copy-done = bf16[1,1024,1024]{2,1,0:T(8,128)(2,1)S(1)} copy-done((bf16[1,1024,1024]{2,1,0:T(8,128)(2,1)S(1)}, bf16[1,1024,1024]{2,1,0:T(8,128)(2,1)}, u32[]{:S(2)}) %copy-start) | copy-done | bytes 2097176
  8.1 0.0 copy-start.3
  8.1 0.9 %copy-done.3 = f32[136,128]{1,0:T(8,128)S(1)} copy-done((f32[136,128]{1,0:T(8,128)S(1)}, f32[136,128]{1,0:T(8,128)}, u32[]{:S(2)}) %copy-start.3) | copy-done | bytes 69656
  9.0 0.0 copy-start.5
  9.0 0.7 copy-done.5
  9.7 0.0 copy-start.1
  9.7 1.7 %prepare.1 = (f32[64,128]{1,0:T(8,128)S(1)}, f32[64,128]{1,0:T(8,128)S(1)}, bf16[128,1024]{1,0:T(8,128)(2,1)S(1)}, s32[8,128]{1,0:T(8,128)S(1)}) custom-call(s32[8,8]{1,0:T(8,128)S(1)} %bitcast.12, f32[136,128]{1,0:T(8,128)S(1)} %copy-done.3, f32[1024,128]{1,0:T(8,128)S(1)} %bitcast.10, bf16[1024,1024]{1,0:T(8,128)(2,1)S(1)} %bitcast.6), custom_call_target="tpu_custom_call" | custom-call | flops 33554432 | bytes 3023104 | tf_op jit(solution)/shard_map/prepare/pallas_call | solution.py:141
  11.4 2.6 %all-to-all-done = bf16[8,128,128]{2,1,0:T(8,128)(2,1)S(1)} async-done(((bf16[8,128,128]{2,1,0:T(8,128)(2,1)}), bf16[8,128,128]{2,1,0:T(8,128)(2,1)S(1)}, u32[]{:S(2)}, u32[]{:S(2)}) %all-to-all-start) | async-done | bytes 262176 | tf_op jit(solution)/shard_map/all_to_all | solution.py:161
  14.0 1.1 %pack.1 = (s16[16,72,128]{2,1,0:T(8,128)(2,1)}, f32[64,128]{1,0:T(8,128)S(1)}) custom-call(f32[64,128]{1,0:T(8,128)S(1)} %get-tuple-element.11.base, bf16[128,1024]{1,0:T(8,128)(2,1)S(1)} %get-tuple-element.12.weights, s32[8,128]{1,0:T(8,128)S(1)} %get-tuple-element.13.places, bf16[1024,128]{1,0:T(8,128)(2,1)S(1)} %bitcast.8), custom_call_target="tpu_custom_call" | custom-call | flops 33554432 | bytes 888832 | tf_op jit(solution)/shard_map/pack/pallas_call | solution.py:141
  15.1 15.2 %all-to-all-start.1 = ((s16[16,72,128]{2,1,0:T(8,128)(2,1)}), s16[16,72,128]{2,1,0:T(8,128)(2,1)S(1)}, u32[]{:S(2)}, u32[]{:S(2)}) async-start(s16[16,72,128]{2,1,0:T(8,128)(2,1)} %get-tuple-element.16), calls=%async_computation.1 | async-start | bytes 589824 | tf_op jit(solution)/shard_map/all_to_all | solution.py:175
  30.3 0.0 copy-done.1
  30.3 0.0 copy-start.4
  30.3 2.0 %subtract.1 = (f32[1024,128]{1,0:T(8,128)}, f32[8,128]{1,0:T(8,128)S(1)}) custom-call(f32[64,128]{1,0:T(8,128)S(1)} %get-tuple-element.10.picked, f32[64,128]{1,0:T(8,128)S(1)} %get-tuple-element.14.left, f32[1024,128]{1,0:T(8,128)S(1)} %bitcast.11, bf16[1024,1024]{1,0:T(8,128)(2,1)S(1)} %bitcast.7, bf16[1024,128]{1,0:T(8,128)(2,1)S(1)} %bitcast.9), custom_call_target="tpu_custom_call" | custom-call | flops 268435456 | bytes 3477504 | tf_op jit(solution)/shard_map/subtract/pallas_call | solution.py:141
  32.3 16.6 %all-to-all-done.1.received = s16[16,72,128]{2,1,0:T(8,128)(2,1)S(1)} async-done(((s16[16,72,128]{2,1,0:T(8,128)(2,1)}), s16[16,72,128]{2,1,0:T(8,128)(2,1)S(1)}, u32[]{:S(2)}, u32[]{:S(2)}) %all-to-all-start.1) | async-done | bytes 294944 | tf_op jit(solution)/shard_map/all_to_all | solution.py:175
  48.9 0.0 copy-done.4
  48.9 1.6 %combine.1 = s16[4,1032,128]{2,1,0:T(8,128)(2,1)S(1)} custom-call(f32[136,128]{1,0:T(8,128)S(1)} %copy-done.4, s16[16,72,128]{2,1,0:T(8,128)(2,1)S(1)} %all-to-all-done.1.received, f32[8,128]{1,0:T(8,128)S(1)} %get-tuple-element.17.after), custom_call_target="tpu_custom_call" | custom-call | bytes 1425408 | tf_op jit(solution)/shard_map/combine/pallas_call | solution.py:141
  50.5 18.2 %all_to_all.15.received = s16[4,1032,128]{2,1,0:T(8,128)(2,1)S(1)} all-to-all(s16[4,1032,128]{2,1,0:T(8,128)(2,1)S(1)} %combine.1), channel_id=1, replica_groups={{0,8,16,24},{32,40,48,56},{64,72,80,88},{96,104,112,120},{128,136,144,1..., dimensions={0} | all-to-all | bytes 2113536 | tf_op jit(solution)/shard_map/all_to_all | solution.py:188
  68.7 1.1 %finish.1 = f32[1024,128]{1,0:T(8,128)} custom-call(s16[4,1032,128]{2,1,0:T(8,128)(2,1)S(1)} %all_to_all.15.received), custom_call_target="tpu_custom_call" | custom-call | bytes 1581056 | tf_op jit(solution)/shard_map/finish/pallas_call | solution.py:141
Async XLA Ops:
  0.6 5.9 %copy-start.2 = (f32[1,1024,128]{2,1,0:T(8,128)S(1)}, f32[1,1024,128]{2,1,0:T(8,128)}, u32[]{:S(2)}) copy-start(f32[1,1024,128]{2,1,0:T(8,128)} %param.5) | copy-start | bytes 1572868
  2.2 11.8 %all-to-all-start = ((bf16[8,128,128]{2,1,0:T(8,128)(2,1)}), bf16[8,128,128]{2,1,0:T(8,128)(2,1)S(1)}, u32[]{:S(2)}, u32[]{:S(2)}) async-start(bf16[8,128,128]{2,1,0:T(8,128)(2,1)} %broadcast_in_dim.11), calls=%async_computation | async-start | bytes 524288 | tf_op jit(solution)/shard_map/all_to_all | solution.py:161
  6.5 1.6 %copy-start = (bf16[1,1024,1024]{2,1,0:T(8,128)(2,1)S(1)}, bf16[1,1024,1024]{2,1,0:T(8,128)(2,1)}, u32[]{:S(2)}) copy-start(bf16[1,1024,1024]{2,1,0:T(8,128)(2,1)} %param.6) | copy-start | bytes 6291460
  8.1 0.9 %copy-start.3 = (f32[136,128]{1,0:T(8,128)S(1)}, f32[136,128]{1,0:T(8,128)}, u32[]{:S(2)}) copy-start(f32[136,128]{1,0:T(8,128)} %constant.2.clone.basis) | copy-start | bytes 208900
  9.0 0.7 copy-start.5
  9.7 20.6 %copy-start.1 = (bf16[1,1024,1024]{2,1,0:T(8,128)(2,1)S(1)}, bf16[1,1024,1024]{2,1,0:T(8,128)(2,1)}, u32[]{:S(2)}) copy-start(bf16[1,1024,1024]{2,1,0:T(8,128)(2,1)} %param.6) | copy-start | bytes 6291460
  15.1 33.9 %all-to-all-start.1 = ((s16[16,72,128]{2,1,0:T(8,128)(2,1)}), s16[16,72,128]{2,1,0:T(8,128)(2,1)S(1)}, u32[]{:S(2)}, u32[]{:S(2)}) async-start(s16[16,72,128]{2,1,0:T(8,128)(2,1)} %get-tuple-element.16), calls=%async_computation.1 | async-start | bytes 589824 | tf_op jit(solution)/shard_map/all_to_all | solution.py:175
  30.3 18.7 %copy-start.4 = (f32[136,128]{1,0:T(8,128)S(1)}, f32[136,128]{1,0:T(8,128)}, u32[]{:S(2)}) copy-start(f32[136,128]{1,0:T(8,128)} %constant.2.clone.basis) | copy-start | bytes 208900

commit v3 on v2

--- a/solution.py
+++ b/solution.py
@@ -118,12 +118,8 @@
         own = dot(basis[:CH, :], 256.0 * sums[:, :CH] + sums[:, CH:], ((0,), (0,)), HIGHEST)
         power = exponent(own, 0)
         powers.append(power)
-        coded = encode(own, power).astype(I16)
-        for y in range(NY):
-            message[y, block(b), :] = coded
-    powers = jnp.concatenate(powers, axis=0).astype(I32).astype(I16)
-    for y in range(NY):
-        message[y, BLOCKS * CH :, :] = powers
+        message[block(b), :] = encode(own, power).astype(I16)
+    message[BLOCKS * CH :, :] = jnp.concatenate(powers, axis=0).astype(I32).astype(I16)
 
 
 def finish(received, update):
@@ -181,11 +177,11 @@
     )
     (message,) = call(
         combine,
-        [array((NY, BLOCKS * CH + BLOCKS, CH), I16)],
+        [array((BLOCKS * CH + BLOCKS, CH), I16)],
         [table, along_z, after],
         limit=8,
     )
-    along_y = lax.all_to_all(message, "rep", 0, 0, axis_index_groups=Y_GROUPS, tiled=True)
+    along_y = lax.all_gather(message, "rep", axis_index_groups=Y_GROUPS)
     (update,) = call(finish, [array((BLOCKS * CH, CH))], [along_y])
     return new_momentum[None], update
 

time: 70.2 us -> 67.6 us (0.963)
  the two profiles are of different devices: /device:TPU:32 before, /device:TPU:64 now
where the time goes in v3:
time: 67.6 us; the launch traced here: 67 us
  starting transfers between devices  19.2 us (28%)
  waiting for transfers between devices  18.4 us (27%)
  blocking collectives  15.7 us (23%)
  Pallas kernels  7.37 us (11%)
  local copies, waits for them, and re-layouts  5.71 us (8%)
  between operations  0.68 us (1%)
    all_to_all x1, waiting for transfers between devices, body(): lax.all_to_all(message, 'rep', 0, 0, axis_index_groups=Z_GROUPS, tiled=True)  16.9 us
    all_gather x1, blocking collectives, body(): along_y = lax.all_gather(message, 'rep', axis_index_groups=Y_GROUPS)  15.7 us
    all_to_all x1, starting transfers between devices, body(): lax.all_to_all(message, 'rep', 0, 0, axis_index_groups=Z_GROUPS, tiled=True)  14.8 us
    pallas_call x5, Pallas kernels, call(): pl.pallas_call(kernel, name=kernel.__name__, out_shape=tuple(out), in_spe...  7.37 us
    all_to_all x1, starting transfers between devices, body(): grads = lax.all_to_all(copies, 'row', 0, 0, tiled=True).reshape(TOK, CH)  4.43 us
    unnamed x14, local copies, waits for them, and re-layouts  4.21 us
    all_to_all x1, waiting for transfers between devices, body(): grads = lax.all_to_all(copies, 'row', 0, 0, tiled=True).reshape(TOK, CH)  1.59 us
    broadcast_in_dim x1, local copies, waits for them, and re-layouts, body(): copies = jnp.broadcast_to(out_grads, (ROWS,) + out_grads.shape[1:])  1.49 us
  transfers between devices with their start and end apart: 2, of which 2 were waited for; matrix products, arithmetic and copies ran while one was open for 0% of the time, Pallas kernels for 6%

profile of v3, /device:TPU:64, one launch (start us, length us, event | category | flops | bytes accessed | tf_op | source)
XLA Modules:
  0.0 67.0 jit_solution(949100294948437811)
XLA Ops:
  0.6 1.5 %broadcast_in_dim.11 = bf16[8,128,128]{2,1,0:T(8,128)(2,1)} broadcast(bf16[128,128]{1,0:T(8,128)(2,1)} %bitcast.15), dimensions={1,2} | broadcast | bytes 294912 | tf_op jit(solution)/shard_map/broadcast_in_dim | solution.py:156
  2.1 0.0 copy-start.3
  2.1 4.4 %all-to-all-start = ((bf16[8,128,128]{2,1,0:T(8,128)(2,1)}), bf16[8,128,128]{2,1,0:T(8,128)(2,1)S(1)}, u32[]{:S(2)}, u32[]{:S(2)}) async-start(bf16[8,128,128]{2,1,0:T(8,128)(2,1)} %broadcast_in_dim.11), calls=%async_computation | async-start | bytes 524288 | tf_op jit(solution)/shard_map/all_to_all | solution.py:157
  6.6 0.0 copy-start
  6.6 1.6 %copy-done = bf16[1,1024,1024]{2,1,0:T(8,128)(2,1)S(1)} copy-done((bf16[1,1024,1024]{2,1,0:T(8,128)(2,1)S(1)}, bf16[1,1024,1024]{2,1,0:T(8,128)(2,1)}, u32[]{:S(2)}) %copy-start) | copy-done | bytes 2097176
  8.2 0.0 copy-start.2
  8.2 1.0 %copy-done.2 = f32[1,1024,128]{2,1,0:T(8,128)S(1)} copy-done((f32[1,1024,128]{2,1,0:T(8,128)S(1)}, f32[1,1024,128]{2,1,0:T(8,128)}, u32[]{:S(2)}) %copy-start.2) | copy-done | bytes 524312
  9.2 0.0 copy-start.4
  9.2 0.9 %copy-done.4 = f32[136,128]{1,0:T(8,128)S(1)} copy-done((f32[136,128]{1,0:T(8,128)S(1)}, f32[136,128]{1,0:T(8,128)}, u32[]{:S(2)}) %copy-start.4) | copy-done | bytes 69656
  10.1 0.0 copy-start.6
  10.1 0.7 %copy-done.6 = s32[1,8,1,8]{3,2,1,0:T(1,128)S(1)} copy-done((s32[1,8,1,8]{3,2,1,0:T(1,128)S(1)}, s32[1,8,1,8]{3,2,1,0:T(1,128)}, u32[]{:S(2)}) %copy-start.6) | copy-done | bytes 280
  10.8 0.0 copy-start.1
  10.8 1.7 %prepare.1 = (f32[64,128]{1,0:T(8,128)S(1)}, f32[64,128]{1,0:T(8,128)S(1)}, bf16[128,1024]{1,0:T(8,128)(2,1)S(1)}, s32[8,128]{1,0:T(8,128)S(1)}) custom-call(s32[8,8]{1,0:T(8,128)S(1)} %bitcast.14, f32[136,128]{1,0:T(8,128)S(1)} %copy-done.4, f32[1024,128]{1,0:T(8,128)S(1)} %bitcast.12, bf16[1024,1024]{1,0:T(8,128)(2,1)S(1)} %bitcast.7), custom_call_target="tpu_custom_call" | custom-call | flops 33554432 | bytes 3023104 | tf_op jit(solution)/shard_map/prepare/pallas_call | solution.py:137
  12.5 0.0 copy-start.5
  12.5 1.6 %all-to-all-done = bf16[8,128,128]{2,1,0:T(8,128)(2,1)S(1)} async-done(((bf16[8,128,128]{2,1,0:T(8,128)(2,1)}), bf16[8,128,128]{2,1,0:T(8,128)(2,1)S(1)}, u32[]{:S(2)}, u32[]{:S(2)}) %all-to-all-start) | async-done | bytes 262176 | tf_op jit(solution)/shard_map/all_to_all | solution.py:157
  14.1 1.1 %pack.1 = (s16[16,72,128]{2,1,0:T(8,128)(2,1)}, f32[64,128]{1,0:T(8,128)S(1)}) custom-call(f32[64,128]{1,0:T(8,128)S(1)} %get-tuple-element.11.base, bf16[128,1024]{1,0:T(8,128)(2,1)S(1)} %get-tuple-element.12.weights, s32[8,128]{1,0:T(8,128)S(1)} %get-tuple-element.13.places, bf16[1024,128]{1,0:T(8,128)(2,1)S(1)} %bitcast.10), custom_call_target="tpu_custom_call" | custom-call | flops 33554432 | bytes 888832 | tf_op jit(solution)/shard_map/pack/pallas_call | solution.py:137
  15.1 14.8 %all-to-all-start.1 = ((s16[16,72,128]{2,1,0:T(8,128)(2,1)}), s16[16,72,128]{2,1,0:T(8,128)(2,1)S(1)}, u32[]{:S(2)}, u32[]{:S(2)}) async-start(s16[16,72,128]{2,1,0:T(8,128)(2,1)} %get-tuple-element.16), calls=%async_computation.1 | async-start | bytes 589824 | tf_op jit(solution)/shard_map/all_to_all | solution.py:171
  29.9 0.0 copy-done.3
  29.9 0.0 copy-done.1
  29.9 2.0 %subtract.1 = (f32[1024,128]{1,0:T(8,128)}, f32[8,128]{1,0:T(8,128)S(1)}) custom-call(f32[64,128]{1,0:T(8,128)S(1)} %get-tuple-element.10.picked, f32[64,128]{1,0:T(8,128)S(1)} %get-tuple-element.14.left, f32[1024,128]{1,0:T(8,128)S(1)} %bitcast.13, bf16[1024,1024]{1,0:T(8,128)(2,1)S(1)} %bitcast.8, bf16[1024,128]{1,0:T(8,128)(2,1)S(1)} %bitcast.11), custom_call_target="tpu_custom_call" | custom-call | flops 268435456 | bytes 3477504 | tf_op jit(solution)/shard_map/subtract/pallas_call | solution.py:137
  31.9 16.9 %all-to-all-done.1.received = s16[16,72,128]{2,1,0:T(8,128)(2,1)S(1)} async-done(((s16[16,72,128]{2,1,0:T(8,128)(2,1)}), s16[16,72,128]{2,1,0:T(8,128)(2,1)S(1)}, u32[]{:S(2)}, u32[]{:S(2)}) %all-to-all-start.1) | async-done | bytes 294944 | tf_op jit(solution)/shard_map/all_to_all | solution.py:171
  48.8 0.0 copy-done.5
  48.8 1.5 %combine.1 = s16[1032,128]{1,0:T(8,128)(2,1)S(1)} custom-call(f32[136,128]{1,0:T(8,128)S(1)} %copy-done.5, s16[16,72,128]{2,1,0:T(8,128)(2,1)S(1)} %all-to-all-done.1.received, f32[8,128]{1,0:T(8,128)S(1)} %get-tuple-element.17.after), custom_call_target="tpu_custom_call" | custom-call | bytes 632832 | tf_op jit(solution)/shard_map/combine/pallas_call | solution.py:137
  50.3 15.7 %all-gather.2 = s16[4128,128]{1,0:T(8,128)(2,1)S(1)} all-gather(s16[1032,128]{1,0:T(8,128)(2,1)S(1)} %combine.1), channel_id=2, replica_groups={{0,8,16,24},{32,40,48,56},{64,72,80,88},{96,104,112,120},{128,136,144,1..., dimensions={0}, use_global_device_ids=true | all-gather | bytes 1320960 | tf_op jit(solution)/shard_map/all_gather | solution.py:184
  66.0 1.1 %finish.1 = f32[1024,128]{1,0:T(8,128)} custom-call(s16[4,1032,128]{2,1,0:T(8,128)(2,1)S(1)} %bitcast.9), custom_call_target="tpu_custom_call" | custom-call | bytes 1581056 | tf_op jit(solution)/shard_map/finish/pallas_call | solution.py:137
Async XLA Ops:
  2.1 27.8 %copy-start.3 = (f32[1,1024,128]{2,1,0:T(8,128)S(1)}, f32[1,1024,128]{2,1,0:T(8,128)}, u32[]{:S(2)}) copy-start(f32[1,1024,128]{2,1,0:T(8,128)} %param.5) | copy-start | bytes 1572868
  2.1 11.9 %all-to-all-start = ((bf16[8,128,128]{2,1,0:T(8,128)(2,1)}), bf16[8,128,128]{2,1,0:T(8,128)(2,1)S(1)}, u32[]{:S(2)}, u32[]{:S(2)}) async-start(bf16[8,128,128]{2,1,0:T(8,128)(2,1)} %broadcast_in_dim.11), calls=%async_computation | async-start | bytes 524288 | tf_op jit(solution)/shard_map/all_to_all | solution.py:157
  6.6 1.6 %copy-start = (bf16[1,1024,1024]{2,1,0:T(8,128)(2,1)S(1)}, bf16[1,1024,1024]{2,1,0:T(8,128)(2,1)}, u32[]{:S(2)}) copy-start(bf16[1,1024,1024]{2,1,0:T(8,128)(2,1)} %param.6) | copy-start | bytes 6291460
  8.2 1.0 %copy-start.2 = (f32[1,1024,128]{2,1,0:T(8,128)S(1)}, f32[1,1024,128]{2,1,0:T(8,128)}, u32[]{:S(2)}) copy-start(f32[1,1024,128]{2,1,0:T(8,128)} %param.5) | copy-start | bytes 1572868
  9.2 0.9 %copy-start.4 = (f32[136,128]{1,0:T(8,128)S(1)}, f32[136,128]{1,0:T(8,128)}, u32[]{:S(2)}) copy-start(f32[136,128]{1,0:T(8,128)} %constant.2.clone.basis) | copy-start | bytes 208900
  10.1 0.7 %copy-start.6 = (s32[1,8,1,8]{3,2,1,0:T(1,128)S(1)}, s32[1,8,1,8]{3,2,1,0:T(1,128)}, u32[]{:S(2)}) copy-start(s32[1,8,1,8]{3,2,1,0:T(1,128)} %param.8) | copy-start | bytes 772
  10.8 19.1 %copy-start.1 = (bf16[1,1024,1024]{2,1,0:T(8,128)(2,1)S(1)}, bf16[1,1024,1024]{2,1,0:T(8,128)(2,1)}, u32[]{:S(2)}) copy-start(bf16[1,1024,1024]{2,1,0:T(8,128)(2,1)} %param.6) | copy-start | bytes 6291460
  12.5 36.3 %copy-start.5 = (f32[136,128]{1,0:T(8,128)S(1)}, f32[136,128]{1,0:T(8,128)}, u32[]{:S(2)}) copy-start(f32[136,128]{1,0:T(8,128)} %constant.2.clone.basis) | copy-start | bytes 208900
  15.1 33.7 %all-to-all-start.1 = ((s16[16,72,128]{2,1,0:T(8,128)(2,1)}), s16[16,72,128]{2,1,0:T(8,128)(2,1)S(1)}, u32[]{:S(2)}, u32[]{:S(2)}) async-start(s16[16,72,128]{2,1,0:T(8,128)(2,1)} %get-tuple-element.16), calls=%async_computation.1 | async-start | bytes 589824 | tf_op jit(solution)/shard_map/all_to_all | solution.py:171

commit v4 on v3

v4 whole, which is shorter than its diff:
```python
import jax
import jax.numpy as jnp
import numpy as np
from jax import lax
from jax.experimental import pallas as pl
from jax.experimental.pallas import tpu as pltpu
from jax.sharding import PartitionSpec as P

CH = 128
K = 8
BLOCKS = 8
PICKS = BLOCKS * K
ROWS = 8
PAIR = 2
TOK = 1024
NZ, NY = 16, 4
MOMENTUM_DECAY = 0.999
AHEAD = 10**10
BITS = 15
TOP = 32767.0
HIGHEST = lax.Precision.HIGHEST
F32, BF16, I32, I16 = jnp.float32, jnp.bfloat16, jnp.int32, jnp.int16

Z_GROUPS = [[z * NY + y for z in range(NZ)] for y in range(NY)]
Y_GROUPS = [[z * NY + y for y in range(NY)] for z in range(NZ)]


def basis_rows():
    frequency = np.arange(CH, dtype=np.float64)[:, None]
    sample = np.arange(CH, dtype=np.float64)[None, :]
    scale = np.where(frequency == 0.0, np.sqrt(1.0 / CH), np.sqrt(2.0 / CH))
    basis = scale * np.cos(np.pi * (2.0 * sample + 1.0) * frequency / (2.0 * CH))
    return np.concatenate([basis, np.zeros((8, CH))]).astype(np.float32)


def dot(a, b, dims, precision=None):
    return lax.dot_general(a, b, (dims, ((), ())), precision=precision, preferred_element_type=F32)


def halves(a):
    high = a.astype(BF16)
    return high, (a - high.astype(F32)).astype(BF16)


def block(b):
    return slice(b * CH, (b + 1) * CH)


def picks(b):
    return slice(b * K, (b + 1) * K)


def exponent(values, axis):
    most = jnp.max(jnp.abs(values), axis=axis, keepdims=True)
    return jnp.ceil(jnp.log2(jnp.maximum(most, 1e-30)) + 0.01)


def encode(values, power):
    scaled = jnp.round(values * jnp.exp2(BITS - power))
    return jnp.clip(scaled, -TOP, TOP).astype(I32)


def spread(out_grads, copies):
    for r in range(ROWS):
        copies[r, :, :] = out_grads[...]


def project(chosen, basis, momentum, inputs, grads, message, picked, left):
    slot = lax.broadcasted_iota(I32, (K, CH), 0)
    lane = lax.broadcasted_iota(I32, (K, CH), 1)
    notes = jnp.zeros((K, CH), I32)
    for i in range(PICKS):
        b, q = i // K, i % K
        row = chosen[b, q]
        picked[i : i + 1, :] = basis[pl.ds(row, 1), :]
        notes = jnp.where((slot == q) & (lane == b), row, notes)
    highs, lows, bases = [], [], []
    for b in range(BLOCKS):
        terms = halves(picked[picks(b), :])
        both = jnp.concatenate(terms, axis=0)
        product = dot(both, inputs[:, block(b)], ((1,), (1,)))
        high, low = halves(product[:K] + product[K:])
        highs.append(high)
        lows.append(low)
        high, low = halves(MOMENTUM_DECAY * momentum[block(b), :])
        product = dot(both, high, ((1,), (0,)))
        bases.append(product[:K] + product[K:] + dot(terms[0], low, ((1,), (0,))))
    product = dot(jnp.concatenate(highs + lows, axis=0), grads[...], ((1,), (0,)))
    own = jnp.concatenate(bases, axis=0) + product[:PICKS] + product[PICKS:]
    left[...] = own
    power = exponent(own, 1)
    codes = encode(own, power).astype(I16)
    for b in range(BLOCKS):
        notes = jnp.where(lane == BLOCKS + b, power[picks(b), :].astype(I32), notes)
    notes = notes.astype(I16)
    for z in range(NZ):
        message[z, :PICKS, :] = codes
        message[z, PICKS:, :] = notes


def subtract(picked, left, momentum, inputs, grads, new_momentum, done):
    grad = dot(inputs[...], grads[...], ((0,), (0,)))
    for b in range(BLOCKS):
        sent = dot(picked[picks(b), :], left[picks(b), :], ((0,), (0,)), HIGHEST)
        new_momentum[block(b), :] = MOMENTUM_DECAY * momentum[block(b), :] + grad[block(b), :] - sent
    done[...] = picked[:8, :]


def combine(basis, received, after, message):
    del after
    notes = received[:, PICKS:, :].astype(I32).astype(F32).reshape(NZ * K, CH).T
    scales = jnp.exp2(notes[BLOCKS : 2 * BLOCKS, :] - BITS)
    rows = lax.broadcasted_iota(I32, (CH, NZ * K), 0).astype(F32)
    high, low = halves(basis[:CH, :].T)
    back = jnp.concatenate([high, low], axis=0)
    powers = []
    for b in range(BLOCKS):
        codes = received[:, picks(b), :].astype(I32).astype(F32).reshape(NZ * K, CH)
        hot = jnp.where(notes[b : b + 1, :] == rows, scales[b : b + 1, :], 0.0).astype(BF16)
        sums = dot(hot, jnp.concatenate(halves(codes), axis=1), ((1,), (0,)))
        own = sums[:, :CH] + sums[:, CH:]
        own_high, own_low = halves(own)
        product = dot(back, own_high, ((1,), (0,)))
        own = product[:CH] + product[CH:] + dot(high, own_low, ((1,), (0,)))
        power = exponent(own, 0)
        powers.append(power)
        message[block(b), :] = encode(own, power).astype(I16)
    message[BLOCKS * CH :, :] = jnp.concatenate(powers, axis=0).astype(I32).astype(I16)


def finish(received, update, total, sems):
    scales = [jnp.exp2(received[y, BLOCKS * CH :, :].astype(I32).astype(F32) - BITS) for y in range(NY)]
    stores = []
    for b in range(BLOCKS):
        parts = [received[y, block(b), :].astype(I32).astype(F32) * scales[y][b : b + 1, :] for y in range(NY)]
        total[block(b), :] = parts[0] + parts[1] + (parts[2] + parts[3])
        if b % PAIR == PAIR - 1:
            done = slice((b + 1 - PAIR) * CH, (b + 1) * CH)
            stores.append(pltpu.make_async_copy(total.at[done, :], update.at[done, :], sems.at[b // PAIR]))
            stores[-1].start()
    for store in stores:
        store.wait()


def call(kernel, out, operands, spaces=None, flops=0, limit=4, scratch=(), result=pltpu.VMEM):
    spaces = spaces or [pltpu.VMEM] * len(operands)
    moved = sum(a.size * a.dtype.itemsize for a in operands) + sum(o.size * o.dtype.itemsize for o in out)
    return pl.pallas_call(
        kernel,
        name=kernel.__name__,
        out_shape=tuple(out),
        in_specs=[pl.BlockSpec(memory_space=s) for s in spaces],
        out_specs=tuple(pl.BlockSpec(memory_space=result) for _ in out),
        scratch_shapes=list(scratch),
        compiler_params=pltpu.CompilerParams(vmem_limit_bytes=int(limit * 2**20)),
        cost_estimate=pl.CostEstimate(flops=flops, bytes_accessed=moved, transcendentals=0),
    )(*operands)


def array(shape, dtype=F32):
    return jax.ShapeDtypeStruct(shape, dtype)


def body(momentum, inputs, out_grads, chosen):
    momentum, inputs = momentum[0], inputs[0]
    table = jnp.asarray(basis_rows())
    (copies,) = call(spread, [array((ROWS,) + out_grads.shape[1:], BF16)], [out_grads[0]], flops=AHEAD)
    grads = lax.all_to_all(copies, "row", 0, 0, tiled=True).reshape(TOK, CH)
    message, picked, left = call(
        project,
        [array((NZ, PICKS + K, CH), I16), array((PICKS, CH)), array((PICKS, CH))],
        [chosen.reshape(BLOCKS, K), table, momentum, inputs, grads],
        spaces=[pltpu.SMEM, pltpu.VMEM, pltpu.VMEM, pltpu.VMEM, pltpu.VMEM],
        flops=2 * 2 * 2 * PICKS * CH * TOK,
    )
    along_z = lax.all_to_all(message, "rep", 0, 0, axis_index_groups=Z_GROUPS, tiled=True)
    new_momentum, after = call(
        subtract,
        [array((BLOCKS * CH, CH)), array((8, CH))],
        [picked, left, momentum, inputs, grads],
        flops=2 * BLOCKS * CH * CH * TOK,
    )
    (message,) = call(
        combine,
        [array((BLOCKS * CH + BLOCKS, CH), I16)],
        [table, along_z, after],
        limit=8,
    )
    along_y = lax.all_gather(message, "rep", axis_index_groups=Y_GROUPS)
    (update,) = call(
        finish,
        [array((BLOCKS * CH, CH))],
        [along_y],
        scratch=[pltpu.VMEM((BLOCKS * CH, CH), F32), pltpu.SemaphoreType.DMA((BLOCKS // PAIR,))],
        result=pl.ANY,
    )
    return new_momentum[None], update


def solution(mesh):
    in_specs = (
        P("rep", "row", None),
        P("rep", None, "row"),
        P("rep", "row", None),
        P("rep", "row", None, None),
    )
    out_specs = (P("rep", "row", None), P("row", None))
    return jax.shard_map(body, mesh=mesh, in_specs=in_specs, out_specs=out_specs, check_vma=False)
```

time: 67.6 us -> 67.5 us (level)
  blocking collectives: 15.7 us -> 27.4 us
  local copies, waits for them, and re-layouts: 5.71 us -> 0.77 us
  starting transfers between devices: 19.2 us -> 14.8 us
  waiting for transfers between devices: 18.4 us -> 16.9 us
    all_to_all x0 -> x1, blocking collectives: none -> 11.7 us  [body(): grads = lax.all_to_all(copies, 'row', 0, 0, tiled=True).reshape(TOK, CH)]
    all_to_all x1 -> x0, starting transfers between devices: 4.43 us -> none  [body(): grads = lax.all_to_all(copies, 'row', 0, 0, tiled=True).reshape(TOK, CH)]
    unnamed x14 -> x10, local copies, waits for them, and re-layouts: 4.21 us -> 0.77 us
    all_to_all x1 -> x0, waiting for transfers between devices: 1.59 us -> none  [body(): grads = lax.all_to_all(copies, 'row', 0, 0, tiled=True).reshape(TOK, CH)]
    broadcast_in_dim x1 -> x0, local copies, waits for them, and re-layouts: 1.49 us -> none  [body(): copies = jnp.broadcast_to(out_grads, (ROWS,) + out_grads.shape[1:])]
  transfers between devices with their start and end apart: 2 -> 1, of which waited for: 2 -> 1; matrix products, arithmetic and copies ran while one was open for 0% -> 0% of each run, Pallas kernels for 6% -> 3%
where the time goes in v4:
time: 67.5 us; the launch traced here: 67.2 us
  blocking collectives  27.4 us (41%)
  waiting for transfers between devices  16.9 us (25%)
  starting transfers between devices  14.8 us (22%)
  Pallas kernels  6.7 us (10%)
  local copies, waits for them, and re-layouts  0.77 us (1%)
    all_to_all x1, waiting for transfers between devices, body(): lax.all_to_all(message, 'rep', 0, 0, axis_index_groups=Z_GROUPS, tiled=True)  16.9 us
    all_gather x1, blocking collectives, body(): along_y = lax.all_gather(message, 'rep', axis_index_groups=Y_GROUPS)  15.7 us
    all_to_all x1, starting transfers between devices, body(): lax.all_to_all(message, 'rep', 0, 0, axis_index_groups=Z_GROUPS, tiled=True)  14.8 us
    all_to_all x1, blocking collectives, body(): grads = lax.all_to_all(copies, 'row', 0, 0, tiled=True).reshape(TOK, CH)  11.7 us
    pallas_call x5, Pallas kernels, call(): pl.pallas_call(kernel, name=kernel.__name__, out_shape=tuple(out), in_spe...  6.7 us
  transfers between devices with their start and end apart: 1, of which 1 were waited for; matrix products, arithmetic and copies ran while one was open for 0% of the time, Pallas kernels for 3%

profile of v4, /device:TPU:64, one launch (start us, length us, event | category | flops | bytes accessed | tf_op | source)
XLA Modules:
  0.0 67.2 jit_solution(1287509110565428318)
XLA Ops:
  0.6 0.0 copy-start.4
  0.6 0.7 %copy-done.4 = bf16[1,128,128]{2,1,0:T(8,128)(2,1)S(1)} copy-done((bf16[1,128,128]{2,1,0:T(8,128)(2,1)S(1)}, bf16[1,128,128]{2,1,0:T(8,128)(2,1)}, u32[]{:S(2)}) %copy-start.4) | copy-done | bytes 32792
  1.4 0.0 copy-start
  1.4 0.0 copy-start.1
  1.4 0.0 copy-start.2
  1.4 0.0 copy-start.3
  1.4 11.7 %all_to_all.10 = bf16[8,128,128]{2,1,0:T(8,128)(2,1)S(1)} all-to-all(bf16[8,128,128]{2,1,0:T(8,128)(2,1)S(1)} %spread.1), channel_id=1, replica_groups=mesh['rep'=64,'row'=8] {'row'}, dimensions={0} | all-to-all | bytes 524288 | tf_op jit(solution)/shard_map/all_to_all | solution.py:168
  13.2 0.0 copy-done
  13.2 0.0 copy-done.1
  13.2 0.0 copy-done.2
  13.2 0.0 copy-done.3
  13.2 2.4 %project.1 = (s16[16,72,128]{2,1,0:T(8,128)(2,1)}, f32[64,128]{1,0:T(8,128)S(1)}, f32[64,128]{1,0:T(8,128)S(1)}) custom-call(s32[8,8]{1,0:T(8,128)S(1)} %bitcast.14, f32[136,128]{1,0:T(8,128)S(1)} %copy-done.2, f32[1024,128]{1,0:T(8,128)S(1)} %bitcast.12, bf16[1024,1024]{1,0:T(8,128)(2,1)S(1)} %bitcast.7, bf16[1024,128]{1,0:T(8,128)(2,1)S(1)} %bitcast.10), custom_call_target="tpu_custom_call" | custom-call | flops 67108864 | bytes 3313920 | tf_op jit(solution)/shard_map/project/pallas_call | solution.py:148
  15.6 14.8 %all-to-all-start.1 = ((s16[16,72,128]{2,1,0:T(8,128)(2,1)}), s16[16,72,128]{2,1,0:T(8,128)(2,1)S(1)}, u32[]{:S(2)}, u32[]{:S(2)}) async-start(s16[16,72,128]{2,1,0:T(8,128)(2,1)} %get-tuple-element.10), calls=%async_computation.1 | async-start | bytes 589824 | tf_op jit(solution)/shard_map/all_to_all | solution.py:176
  30.4 2.0 %subtract.1 = (f32[1024,128]{1,0:T(8,128)}, f32[8,128]{1,0:T(8,128)S(1)}) custom-call(f32[64,128]{1,0:T(8,128)S(1)} %get-tuple-element.7.picked, f32[64,128]{1,0:T(8,128)S(1)} %get-tuple-element.8.left, f32[1024,128]{1,0:T(8,128)S(1)} %bitcast.13, bf16[1024,1024]{1,0:T(8,128)(2,1)S(1)} %bitcast.8, bf16[1024,128]{1,0:T(8,128)(2,1)S(1)} %bitcast.11), custom_call_target="tpu_custom_call" | custom-call | flops 268435456 | bytes 3477504 | tf_op jit(solution)/shard_map/subtract/pallas_call | solution.py:148
  32.4 16.9 %all-to-all-done.1.received = s16[16,72,128]{2,1,0:T(8,128)(2,1)S(1)} async-done(((s16[16,72,128]{2,1,0:T(8,128)(2,1)}), s16[16,72,128]{2,1,0:T(8,128)(2,1)S(1)}, u32[]{:S(2)}, u32[]{:S(2)}) %all-to-all-start.1) | async-done | bytes 294944 | tf_op jit(solution)/shard_map/all_to_all | solution.py:176
  49.3 1.3 %combine.1 = s16[1032,128]{1,0:T(8,128)(2,1)S(1)} custom-call(f32[136,128]{1,0:T(8,128)S(1)} %copy-done.2, s16[16,72,128]{2,1,0:T(8,128)(2,1)S(1)} %all-to-all-done.1.received, f32[8,128]{1,0:T(8,128)S(1)} %get-tuple-element.11.after), custom_call_target="tpu_custom_call" | custom-call | bytes 632832 | tf_op jit(solution)/shard_map/combine/pallas_call | solution.py:148
  50.5 15.7 %all-gather.2 = s16[4128,128]{1,0:T(8,128)(2,1)S(1)} all-gather(s16[1032,128]{1,0:T(8,128)(2,1)S(1)} %combine.1), channel_id=2, replica_groups={{0,8,16,24},{32,40,48,56},{64,72,80,88},{96,104,112,120},{128,136,144,1..., dimensions={0}, use_global_device_ids=true | all-gather | bytes 1320960 | tf_op jit(solution)/shard_map/all_gather | solution.py:189
  66.2 1.0 %finish.1 = f32[1024,128]{1,0:T(8,128)} custom-call(s16[4,1032,128]{2,1,0:T(8,128)(2,1)S(1)} %bitcast.9), custom_call_target="tpu_custom_call" | custom-call | bytes 1581056 | tf_op jit(solution)/shard_map/finish/pallas_call | solution.py:148
  (1 shorter events, 0.0 us)
Async XLA Ops:
  0.6 0.8 %copy-start.4 = (bf16[1,128,128]{2,1,0:T(8,128)(2,1)S(1)}, bf16[1,128,128]{2,1,0:T(8,128)(2,1)}, u32[]{:S(2)}) copy-start(bf16[1,128,128]{2,1,0:T(8,128)(2,1)} %param.7) | copy-start | bytes 98308
  1.4 11.8 %copy-start = (bf16[1,1024,1024]{2,1,0:T(8,128)(2,1)S(1)}, bf16[1,1024,1024]{2,1,0:T(8,128)(2,1)}, u32[]{:S(2)}) copy-start(bf16[1,1024,1024]{2,1,0:T(8,128)(2,1)} %param.6) | copy-start | bytes 6291460
  1.4 11.8 %copy-start.1 = (f32[1,1024,128]{2,1,0:T(8,128)S(1)}, f32[1,1024,128]{2,1,0:T(8,128)}, u32[]{:S(2)}) copy-start(f32[1,1024,128]{2,1,0:T(8,128)} %param.5) | copy-start | bytes 1572868
  1.4 11.8 %copy-start.2 = (f32[136,128]{1,0:T(8,128)S(1)}, f32[136,128]{1,0:T(8,128)}, u32[]{:S(2)}) copy-start(f32[136,128]{1,0:T(8,128)} %constant.2.clone.basis) | copy-start | bytes 208900
  1.4 11.8 %copy-start.3 = (s32[1,8,1,8]{3,2,1,0:T(1,128)S(1)}, s32[1,8,1,8]{3,2,1,0:T(1,128)}, u32[]{:S(2)}) copy-start(s32[1,8,1,8]{3,2,1,0:T(1,128)} %param.8) | copy-start | bytes 772
  15.6 33.7 %all-to-all-start.1 = ((s16[16,72,128]{2,1,0:T(8,128)(2,1)}), s16[16,72,128]{2,1,0:T(8,128)(2,1)S(1)}, u32[]{:S(2)}, u32[]{:S(2)}) async-start(s16[16,72,128]{2,1,0:T(8,128)(2,1)} %get-tuple-element.10), calls=%async_computation.1 | async-start | bytes 589824 | tf_op jit(solution)/shard_map/all_to_all | solution.py:176

commit v5 on v4

--- a/solution.py
+++ b/solution.py
@@ -18,6 +18,8 @@
 AHEAD = 10**10
 BITS = 15
 TOP = 32767.0
+SHIFT = 2**16
+WORDS = PICKS // 2
 HIGHEST = lax.Precision.HIGHEST
 F32, BF16, I32, I16 = jnp.float32, jnp.bfloat16, jnp.int32, jnp.int16
 
@@ -65,37 +67,47 @@
         copies[r, :, :] = out_grads[...]
 
 
-def project(chosen, basis, momentum, inputs, grads, message, picked, left):
-    slot = lax.broadcasted_iota(I32, (K, CH), 0)
-    lane = lax.broadcasted_iota(I32, (K, CH), 1)
-    notes = jnp.zeros((K, CH), I32)
-    for i in range(PICKS):
-        b, q = i // K, i % K
-        row = chosen[b, q]
-        picked[i : i + 1, :] = basis[pl.ds(row, 1), :]
-        notes = jnp.where((slot == q) & (lane == b), row, notes)
+def project(chosen, basis, momentum, inputs, grads, message, picked, left, coded, sems):
+    wide = jnp.concatenate([chosen[...], jnp.zeros((BLOCKS, CH - K), I32)], axis=1)
+    notes = jnp.sum(pltpu.roll(wide, 0, 1, stride=K, stride_axis=0), axis=0, keepdims=True)
+    numbers = jnp.where(lax.broadcasted_iota(I32, (1, CH), 1) < PICKS, notes, CH)
+    hot = jnp.where(numbers == lax.broadcasted_iota(I32, (CH, CH), 0), 1.0, 0.0).astype(BF16)
+    basis_high, basis_low = halves(basis[:CH, :])
+    own_high = dot(hot, basis_high, ((0,), (0,)))[:PICKS].astype(BF16)
+    own_low = dot(hot, basis_low, ((0,), (0,)))[:PICKS].astype(BF16)
+    picked[...] = own_high.astype(F32) + own_low.astype(F32)
     highs, lows, bases = [], [], []
-    for b in range(BLOCKS):
-        terms = halves(picked[picks(b), :])
-        both = jnp.concatenate(terms, axis=0)
-        product = dot(both, inputs[:, block(b)], ((1,), (1,)))
-        high, low = halves(product[:K] + product[K:])
-        highs.append(high)
-        lows.append(low)
-        high, low = halves(MOMENTUM_DECAY * momentum[block(b), :])
-        product = dot(both, high, ((1,), (0,)))
-        bases.append(product[:K] + product[K:] + dot(terms[0], low, ((1,), (0,))))
+    for b in range(0, BLOCKS, 2):
+        pair = slice(b * CH, (b + 2) * CH)
+        first = jnp.concatenate([own_high[picks(b)], own_low[picks(b)]], axis=0)
+        second = jnp.concatenate([own_high[picks(b + 1)], own_low[picks(b + 1)]], axis=0)
+        none = jnp.zeros_like(first)
+        both = jnp.concatenate([jnp.concatenate([first, none], axis=1), jnp.concatenate([none, second], axis=1)], axis=0)
+        product = dot(both, inputs[:, pair], ((1,), (1,)))
+        moment_high, moment_low = halves(MOMENTUM_DECAY * momentum[pair, :])
+        known = dot(both, moment_high, ((1,), (0,)))
+        rest = dot(both, moment_low, ((1,), (0,)))
+        for top in (0, 2 * K):
+            high, low = halves(product[top : top + K] + product[top + K : top + 2 * K])
+            highs.append(high)
+            lows.append(low)
+            bases.append(known[top : top + K] + known[top + K : top + 2 * K] + rest[top : top + K])
     product = dot(jnp.concatenate(highs + lows, axis=0), grads[...], ((1,), (0,)))
     own = jnp.concatenate(bases, axis=0) + product[:PICKS] + product[PICKS:]
     left[...] = own
     power = exponent(own, 1)
-    codes = encode(own, power).astype(I16)
-    for b in range(BLOCKS):
-        notes = jnp.where(lane == BLOCKS + b, power[picks(b), :].astype(I32), notes)
-    notes = notes.astype(I16)
-    for z in range(NZ):
-        message[z, :PICKS, :] = codes
-        message[z, PICKS:, :] = notes
+    codes = encode(own, power)
+    words = [codes[picks(b), :] + codes[picks(b + 1), :] * SHIFT for b in range(0, BLOCKS, 2)]
+    place = lax.broadcasted_iota(I32, (PICKS, CH), 1) == lax.broadcasted_iota(I32, (PICKS, CH), 0) + PICKS
+    notes = notes + jnp.sum(jnp.where(place, power, 0.0), axis=0, keepdims=True).astype(I32)
+    for i, word in enumerate(words):
+        coded[picks(i), 0, :] = word
+    coded[WORDS:, 0, :] = notes
+    stores = [pltpu.make_async_copy(coded, message.at[z], sems.at[z]) for z in range(NZ)]
+    for store in stores:
+        store.start()
+    for store in stores:
+        store.wait()
 
 
 def subtract(picked, left, momentum, inputs, grads, new_momentum, done):
@@ -108,23 +120,33 @@
 
 def combine(basis, received, after, message):
     del after
-    notes = received[:, PICKS:, :].astype(I32).astype(F32).reshape(NZ * K, CH).T
-    scales = jnp.exp2(notes[BLOCKS : 2 * BLOCKS, :] - BITS)
+    notes = jnp.concatenate([received[:, WORDS, 0, :].astype(F32)] * K, axis=0).T
+    own_slot = lax.broadcasted_iota(I32, (K, CH), 1) // NZ == lax.broadcasted_iota(I32, (K, CH), 0)
+    notes = [jnp.sum(jnp.where(own_slot, notes[picks(i), :], 0.0), axis=0, keepdims=True) for i in range(2 * BLOCKS)]
+    scales = jnp.exp2(jnp.concatenate(notes[BLOCKS:], axis=0) - BITS)
     rows = lax.broadcasted_iota(I32, (CH, NZ * K), 0).astype(F32)
     high, low = halves(basis[:CH, :].T)
     back = jnp.concatenate([high, low], axis=0)
+    codes = []
+    for i in range(0, WORDS, K):
+        words = jnp.concatenate([received[:, i + q, 0, :] for q in range(K)], axis=0)
+        even = lax.shift_right_arithmetic(lax.shift_left(words, 16), 16)
+        codes += [even, lax.shift_right_arithmetic(words - even, 16)]
     powers = []
-    for b in range(BLOCKS):
-        codes = received[:, picks(b), :].astype(I32).astype(F32).reshape(NZ * K, CH)
-        hot = jnp.where(notes[b : b + 1, :] == rows, scales[b : b + 1, :], 0.0).astype(BF16)
-        sums = dot(hot, jnp.concatenate(halves(codes), axis=1), ((1,), (0,)))
-        own = sums[:, :CH] + sums[:, CH:]
-        own_high, own_low = halves(own)
+    for b in range(0, BLOCKS, 2):
+        pair = []
+        for i in (b, b + 1):
+            hot = jnp.where(notes[i] == rows, scales[i : i + 1, :], 0.0).astype(BF16)
+            sums = dot(hot, jnp.concatenate(halves(codes[i].astype(F32)), axis=1), ((1,), (0,)))
+            pair.append(sums[:, :CH] + sums[:, CH:])
+        own_high, own_low = halves(jnp.concatenate(pair, axis=1))
         product = dot(back, own_high, ((1,), (0,)))
         own = product[:CH] + product[CH:] + dot(high, own_low, ((1,), (0,)))
         power = exponent(own, 0)
-        powers.append(power)
-        message[block(b), :] = encode(own, power).astype(I16)
+        coded = encode(own, power).astype(I16)
+        for i in (0, 1):
+            powers.append(power[:, i * CH : (i + 1) * CH])
+            message[block(b + i), :] = coded[:, i * CH : (i + 1) * CH]
     message[BLOCKS * CH :, :] = jnp.concatenate(powers, axis=0).astype(I32).astype(I16)
 
 
@@ -142,15 +164,16 @@
         store.wait()
 
 
-def call(kernel, out, operands, spaces=None, flops=0, limit=4, scratch=(), result=pltpu.VMEM):
+def call(kernel, out, operands, spaces=None, flops=0, limit=4, scratch=(), results=None):
     spaces = spaces or [pltpu.VMEM] * len(operands)
+    results = results or [pltpu.VMEM] * len(out)
     moved = sum(a.size * a.dtype.itemsize for a in operands) + sum(o.size * o.dtype.itemsize for o in out)
     return pl.pallas_call(
         kernel,
         name=kernel.__name__,
         out_shape=tuple(out),
         in_specs=[pl.BlockSpec(memory_space=s) for s in spaces],
-        out_specs=tuple(pl.BlockSpec(memory_space=result) for _ in out),
+        out_specs=tuple(pl.BlockSpec(memory_space=s) for s in results),
         scratch_shapes=list(scratch),
         compiler_params=pltpu.CompilerParams(vmem_limit_bytes=int(limit * 2**20)),
         cost_estimate=pl.CostEstimate(flops=flops, bytes_accessed=moved, transcendentals=0),
@@ -168,10 +191,11 @@
     grads = lax.all_to_all(copies, "row", 0, 0, tiled=True).reshape(TOK, CH)
     message, picked, left = call(
         project,
-        [array((NZ, PICKS + K, CH), I16), array((PICKS, CH)), array((PICKS, CH))],
+        [array((NZ, WORDS + 1, 1, CH), I32), array((PICKS, CH)), array((PICKS, CH))],
         [chosen.reshape(BLOCKS, K), table, momentum, inputs, grads],
-        spaces=[pltpu.SMEM, pltpu.VMEM, pltpu.VMEM, pltpu.VMEM, pltpu.VMEM],
         flops=2 * 2 * 2 * PICKS * CH * TOK,
+        scratch=[pltpu.VMEM((WORDS + 1, 1, CH), I32), pltpu.SemaphoreType.DMA((NZ,))],
+        results=[pl.ANY, pltpu.VMEM, pltpu.VMEM],
     )
     along_z = lax.all_to_all(message, "rep", 0, 0, axis_index_groups=Z_GROUPS, tiled=True)
     new_momentum, after = call(
@@ -192,7 +216,7 @@
         [array((BLOCKS * CH, CH))],
         [along_y],
         scratch=[pltpu.VMEM((BLOCKS * CH, CH), F32), pltpu.SemaphoreType.DMA((BLOCKS // PAIR,))],
-        result=pl.ANY,
+        results=[pl.ANY],
     )
     return new_momentum[None], update
 

time: 67.5 us -> 66.1 us (0.979)
  waiting for transfers between devices: 16.9 us -> 16.2 us
where the time goes in v5:
time: 66.1 us; the launch traced here: 65.8 us
  blocking collectives  27.3 us (41%)
  waiting for transfers between devices  16.2 us (25%)
  starting transfers between devices  14.8 us (22%)
  Pallas kernels  6.06 us (9%)
  local copies, waits for them, and re-layouts  0.77 us (1%)
  between operations  0.68 us (1%)
    all_to_all x1, waiting for transfers between devices, body(): lax.all_to_all(message, 'rep', 0, 0, axis_index_groups=Z_GROUPS, tiled=True)  16.2 us
    all_gather x1, blocking collectives, body(): along_y = lax.all_gather(message, 'rep', axis_index_groups=Y_GROUPS)  15.6 us
    all_to_all x1, starting transfers between devices, body(): lax.all_to_all(message, 'rep', 0, 0, axis_index_groups=Z_GROUPS, tiled=True)  14.8 us
    all_to_all x1, blocking collectives, body(): grads = lax.all_to_all(copies, 'row', 0, 0, tiled=True).reshape(TOK, CH)  11.7 us
    pallas_call x5, Pallas kernels, call(): pl.pallas_call(kernel, name=kernel.__name__, out_shape=tuple(out), in_spe...  6.06 us
  transfers between devices with their start and end apart: 1, of which 1 were waited for; matrix products, arithmetic and copies ran while one was open for 0% of the time, Pallas kernels for 3%

profile of v5, /device:TPU:64, one launch (start us, length us, event | category | flops | bytes accessed | tf_op | source)
XLA Modules:
  0.0 65.8 jit_solution(9578023015265978385)
XLA Ops:
  0.6 0.0 copy-start.4
  0.6 0.7 %copy-done.4 = bf16[1,128,128]{2,1,0:T(8,128)(2,1)S(1)} copy-done((bf16[1,128,128]{2,1,0:T(8,128)(2,1)S(1)}, bf16[1,128,128]{2,1,0:T(8,128)(2,1)}, u32[]{:S(2)}) %copy-start.4) | copy-done | bytes 32792
  1.4 0.0 copy-start
  1.4 0.0 copy-start.1
  1.4 0.0 copy-start.2
  1.4 0.0 copy-start.3
  1.4 11.7 %all_to_all.10 = bf16[8,128,128]{2,1,0:T(8,128)(2,1)S(1)} all-to-all(bf16[8,128,128]{2,1,0:T(8,128)(2,1)S(1)} %spread.1), channel_id=1, replica_groups=mesh['rep'=64,'row'=8] {'row'}, dimensions={0} | all-to-all | bytes 524288 | tf_op jit(solution)/shard_map/all_to_all | solution.py:191
  13.2 0.0 copy-done
  13.2 0.0 copy-done.1
  13.2 0.0 copy-done.2
  13.2 0.0 copy-done.3
  13.2 2.1 %project.1 = (s32[16,33,1,128]{3,2,1,0:T(1,128)}, f32[64,128]{1,0:T(8,128)S(1)}, f32[64,128]{1,0:T(8,128)S(1)}) custom-call(s32[8,8]{1,0:T(8,128)S(1)} %bitcast.14, f32[136,128]{1,0:T(8,128)S(1)} %copy-done.2, f32[1024,128]{1,0:T(8,128)S(1)} %bitcast.12, bf16[1024,1024]{1,0:T(8,128)(2,1)S(1)} %bitcast.7, bf16[1024,128]{1,0:T(8,128)(2,1)S(1)} %bitcast.10), custom_call_target="tpu_custom_call" | custom-call | flops 67108864 | bytes 3289344 | tf_op jit(solution)/shard_map/project/pallas_call | solution.py:171
  15.3 14.8 %all-to-all-start.1 = ((s32[16,33,1,128]{3,2,1,0:T(1,128)}), s32[16,33,1,128]{3,2,1,0:T(1,128)S(1)}, u32[]{:S(2)}, u32[]{:S(2)}) async-start(s32[16,33,1,128]{3,2,1,0:T(1,128)} %get-tuple-element.10), calls=%async_computation.1 | async-start | bytes 540672 | tf_op jit(solution)/shard_map/all_to_all | solution.py:200
  30.1 2.0 %subtract.1 = (f32[1024,128]{1,0:T(8,128)}, f32[8,128]{1,0:T(8,128)S(1)}) custom-call(f32[64,128]{1,0:T(8,128)S(1)} %get-tuple-element.7.picked, f32[64,128]{1,0:T(8,128)S(1)} %get-tuple-element.8.left, f32[1024,128]{1,0:T(8,128)S(1)} %bitcast.13, bf16[1024,1024]{1,0:T(8,128)(2,1)S(1)} %bitcast.8, bf16[1024,128]{1,0:T(8,128)(2,1)S(1)} %bitcast.11), custom_call_target="tpu_custom_call" | custom-call | flops 268435456 | bytes 3477504 | tf_op jit(solution)/shard_map/subtract/pallas_call | solution.py:171
  32.1 16.2 %all-to-all-done.1.received = s32[16,33,1,128]{3,2,1,0:T(1,128)S(1)} async-done(((s32[16,33,1,128]{3,2,1,0:T(1,128)}), s32[16,33,1,128]{3,2,1,0:T(1,128)S(1)}, u32[]{:S(2)}, u32[]{:S(2)}) %all-to-all-start.1) | async-done | bytes 270368 | tf_op jit(solution)/shard_map/all_to_all | solution.py:200
  48.3 1.0 %combine.1 = s16[1032,128]{1,0:T(8,128)(2,1)S(1)} custom-call(f32[136,128]{1,0:T(8,128)S(1)} %copy-done.2, s32[16,33,1,128]{3,2,1,0:T(1,128)S(1)} %all-to-all-done.1.received, f32[8,128]{1,0:T(8,128)S(1)} %get-tuple-element.11.after), custom_call_target="tpu_custom_call" | custom-call | bytes 608256 | tf_op jit(solution)/shard_map/combine/pallas_call | solution.py:171
  49.3 15.6 %all-gather.2 = s16[4128,128]{1,0:T(8,128)(2,1)S(1)} all-gather(s16[1032,128]{1,0:T(8,128)(2,1)S(1)} %combine.1), channel_id=2, replica_groups={{0,8,16,24},{32,40,48,56},{64,72,80,88},{96,104,112,120},{128,136,144,1..., dimensions={0}, use_global_device_ids=true | all-gather | bytes 1320960 | tf_op jit(solution)/shard_map/all_gather | solution.py:213
  64.9 1.0 %finish.1 = f32[1024,128]{1,0:T(8,128)} custom-call(s16[4,1032,128]{2,1,0:T(8,128)(2,1)S(1)} %bitcast.9), custom_call_target="tpu_custom_call" | custom-call | bytes 1581056 | tf_op jit(solution)/shard_map/finish/pallas_call | solution.py:171
  (1 shorter events, 0.0 us)
Async XLA Ops:
  0.6 0.8 %copy-start.4 = (bf16[1,128,128]{2,1,0:T(8,128)(2,1)S(1)}, bf16[1,128,128]{2,1,0:T(8,128)(2,1)}, u32[]{:S(2)}) copy-start(bf16[1,128,128]{2,1,0:T(8,128)(2,1)} %param.7) | copy-start | bytes 98308
  1.4 11.8 %copy-start = (bf16[1,1024,1024]{2,1,0:T(8,128)(2,1)S(1)}, bf16[1,1024,1024]{2,1,0:T(8,128)(2,1)}, u32[]{:S(2)}) copy-start(bf16[1,1024,1024]{2,1,0:T(8,128)(2,1)} %param.6) | copy-start | bytes 6291460
  1.4 11.8 %copy-start.1 = (f32[1,1024,128]{2,1,0:T(8,128)S(1)}, f32[1,1024,128]{2,1,0:T(8,128)}, u32[]{:S(2)}) copy-start(f32[1,1024,128]{2,1,0:T(8,128)} %param.5) | copy-start | bytes 1572868
  1.4 11.8 %copy-start.2 = (f32[136,128]{1,0:T(8,128)S(1)}, f32[136,128]{1,0:T(8,128)}, u32[]{:S(2)}) copy-start(f32[136,128]{1,0:T(8,128)} %constant.2.clone.basis) | copy-start | bytes 208900
  1.4 11.8 %copy-start.3 = (s32[1,8,1,8]{3,2,1,0:T(1,128)S(1)}, s32[1,8,1,8]{3,2,1,0:T(1,128)}, u32[]{:S(2)}) copy-start(s32[1,8,1,8]{3,2,1,0:T(1,128)} %param.8) | copy-start | bytes 772
  15.3 33.0 %all-to-all-start.1 = ((s32[16,33,1,128]{3,2,1,0:T(1,128)}), s32[16,33,1,128]{3,2,1,0:T(1,128)S(1)}, u32[]{:S(2)}, u32[]{:S(2)}) async-start(s32[16,33,1,128]{3,2,1,0:T(1,128)} %get-tuple-element.10), calls=%async_computation.1 | async-start | bytes 540672 | tf_op jit(solution)/shard_map/all_to_all | solution.py:200

commit v6 on v5

--- a/solution.py
+++ b/solution.py
@@ -67,7 +67,7 @@
         copies[r, :, :] = out_grads[...]
 
 
-def project(chosen, basis, momentum, inputs, grads, message, picked, left, coded, sems):
+def project(chosen, basis, momentum, inputs, grads, message, picked, left):
     wide = jnp.concatenate([chosen[...], jnp.zeros((BLOCKS, CH - K), I32)], axis=1)
     notes = jnp.sum(pltpu.roll(wide, 0, 1, stride=K, stride_axis=0), axis=0, keepdims=True)
     numbers = jnp.where(lax.broadcasted_iota(I32, (1, CH), 1) < PICKS, notes, CH)
@@ -100,26 +100,25 @@
     words = [codes[picks(b), :] + codes[picks(b + 1), :] * SHIFT for b in range(0, BLOCKS, 2)]
     place = lax.broadcasted_iota(I32, (PICKS, CH), 1) == lax.broadcasted_iota(I32, (PICKS, CH), 0) + PICKS
     notes = notes + jnp.sum(jnp.where(place, power, 0.0), axis=0, keepdims=True).astype(I32)
-    for i, word in enumerate(words):
-        coded[picks(i), 0, :] = word
-    coded[WORDS:, 0, :] = notes
-    stores = [pltpu.make_async_copy(coded, message.at[z], sems.at[z]) for z in range(NZ)]
-    for store in stores:
-        store.start()
-    for store in stores:
-        store.wait()
-
-
-def subtract(picked, left, momentum, inputs, grads, new_momentum, done):
-    grad = dot(inputs[...], grads[...], ((0,), (0,)))
+    for z in range(NZ):
+        for i, word in enumerate(words):
+            message[z, picks(i), 0, :] = word
+        message[z, WORDS:, 0, :] = notes
+
+
+def combine(basis, received, picked, left, momentum, inputs, grads, message, new_momentum, moment, sems):
+    grad = dot(grads[...], inputs[...], ((0,), (0,)))
+    stores = []
     for b in range(BLOCKS):
-        sent = dot(picked[picks(b), :], left[picks(b), :], ((0,), (0,)), HIGHEST)
-        new_momentum[block(b), :] = MOMENTUM_DECAY * momentum[block(b), :] + grad[block(b), :] - sent
-    done[...] = picked[:8, :]
-
-
-def combine(basis, received, after, message):
-    del after
+        own_high, own_low = halves(picked[picks(b), :])
+        left_high, left_low = halves(left[picks(b), :])
+        own = jnp.concatenate([own_high, own_low, own_high], axis=0)
+        sent = dot(own, jnp.concatenate([left_high, left_high, left_low], axis=0), ((0,), (0,)))
+        moment[block(b), :] = MOMENTUM_DECAY * momentum[block(b), :] + grad[:, block(b)].T - sent
+        if b % PAIR == PAIR - 1:
+            done = slice((b + 1 - PAIR) * CH, (b + 1) * CH)
+            stores.append(pltpu.make_async_copy(moment.at[done, :], new_momentum.at[done, :], sems.at[b // PAIR]))
+            stores[-1].start()
     notes = jnp.concatenate([received[:, WORDS, 0, :].astype(F32)] * K, axis=0).T
     own_slot = lax.broadcasted_iota(I32, (K, CH), 1) // NZ == lax.broadcasted_iota(I32, (K, CH), 0)
     notes = [jnp.sum(jnp.where(own_slot, notes[picks(i), :], 0.0), axis=0, keepdims=True) for i in range(2 * BLOCKS)]
@@ -148,6 +147,8 @@
             powers.append(power[:, i * CH : (i + 1) * CH])
             message[block(b + i), :] = coded[:, i * CH : (i + 1) * CH]
     message[BLOCKS * CH :, :] = jnp.concatenate(powers, axis=0).astype(I32).astype(I16)
+    for store in stores:
+        store.wait()
 
 
 def finish(received, update, total, sems):
@@ -194,21 +195,16 @@
         [array((NZ, WORDS + 1, 1, CH), I32), array((PICKS, CH)), array((PICKS, CH))],
         [chosen.reshape(BLOCKS, K), table, momentum, inputs, grads],
         flops=2 * 2 * 2 * PICKS * CH * TOK,
-        scratch=[pltpu.VMEM((WORDS + 1, 1, CH), I32), pltpu.SemaphoreType.DMA((NZ,))],
-        results=[pl.ANY, pltpu.VMEM, pltpu.VMEM],
     )
     along_z = lax.all_to_all(message, "rep", 0, 0, axis_index_groups=Z_GROUPS, tiled=True)
-    new_momentum, after = call(
-        subtract,
-        [array((BLOCKS * CH, CH)), array((8, CH))],
-        [picked, left, momentum, inputs, grads],
+    message, new_momentum = call(
+        combine,
+        [array((BLOCKS * CH + BLOCKS, CH), I16), array((BLOCKS * CH, CH))],
+        [table, along_z, picked, left, momentum, inputs, grads],
+        limit=8,
         flops=2 * BLOCKS * CH * CH * TOK,
-    )
-    (message,) = call(
-        combine,
-        [array((BLOCKS * CH + BLOCKS, CH), I16)],
-        [table, along_z, after],
-        limit=8,
+        scratch=[pltpu.VMEM((BLOCKS * CH, CH), F32), pltpu.SemaphoreType.DMA((BLOCKS // PAIR,))],
+        results=[pltpu.VMEM, pl.ANY],
     )
     along_y = lax.all_gather(message, "rep", axis_index_groups=Y_GROUPS)
     (update,) = call(

time: 66.1 us -> 65.6 us (level)
  blocking collectives: 27.3 us -> 60.2 us
  waiting for transfers between devices: 16.2 us -> 0 us
  starting transfers between devices: 14.8 us -> 0 us
  Pallas kernels: 6.06 us -> 3.76 us
    all_to_all x0 -> x1, blocking collectives: none -> 32.8 us  [body(): lax.all_to_all(message, 'rep', 0, 0, axis_index_groups=Z_GROUPS, tiled=True)]
    all_to_all x1 -> x0, waiting for transfers between devices: 16.2 us -> none  [body(): lax.all_to_all(message, 'rep', 0, 0, axis_index_groups=Z_GROUPS, tiled=True)]
    all_to_all x1 -> x0, starting transfers between devices: 14.8 us -> none  [body(): lax.all_to_all(message, 'rep', 0, 0, axis_index_groups=Z_GROUPS, tiled=True)]
    pallas_call x5 -> x4, Pallas kernels: 6.06 us -> 3.76 us  [call(): pl.pallas_call(kernel, name=kernel.__name__, out_shape=tuple(out), in_spe...]
  transfers between devices with their start and end apart: 1 -> 0, of which waited for: 1 -> 0; matrix products, arithmetic and copies ran while one was open for 0% -> 0% of each run, Pallas kernels for 3% -> 0%
where the time goes in v6:
time: 65.6 us; the launch traced here: 65.4 us
  blocking collectives  60.2 us (92%)
  Pallas kernels  3.76 us (6%)
  local copies, waits for them, and re-layouts  0.77 us (1%)
  between operations  0.68 us (1%)
    all_to_all x1, blocking collectives, body(): lax.all_to_all(message, 'rep', 0, 0, axis_index_groups=Z_GROUPS, tiled=True)  32.8 us
    all_gather x1, blocking collectives, body(): along_y = lax.all_gather(message, 'rep', axis_index_groups=Y_GROUPS)  15.7 us
    all_to_all x1, blocking collectives, body(): grads = lax.all_to_all(copies, 'row', 0, 0, tiled=True).reshape(TOK, CH)  11.7 us
    pallas_call x4, Pallas kernels, call(): pl.pallas_call(kernel, name=kernel.__name__, out_shape=tuple(out), in_spe...  3.76 us

profile of v6, /device:TPU:64, one launch (start us, length us, event | category | flops | bytes accessed | tf_op | source)
XLA Modules:
  0.0 65.4 jit_solution(13472342685168816633)
XLA Ops:
  0.6 0.0 copy-start.4
  0.6 0.7 %copy-done.4 = bf16[1,128,128]{2,1,0:T(8,128)(2,1)S(1)} copy-done((bf16[1,128,128]{2,1,0:T(8,128)(2,1)S(1)}, bf16[1,128,128]{2,1,0:T(8,128)(2,1)}, u32[]{:S(2)}) %copy-start.4) | copy-done | bytes 32792
  1.4 0.0 copy-start
  1.4 0.0 copy-start.1
  1.4 0.0 copy-start.2
  1.4 0.0 copy-start.3
  1.4 11.7 %all_to_all.10 = bf16[8,128,128]{2,1,0:T(8,128)(2,1)S(1)} all-to-all(bf16[8,128,128]{2,1,0:T(8,128)(2,1)S(1)} %spread.1), channel_id=1, replica_groups=mesh['rep'=64,'row'=8] {'row'}, dimensions={0} | all-to-all | bytes 524288 | tf_op jit(solution)/shard_map/all_to_all | solution.py:192
  13.2 0.0 copy-done
  13.2 0.0 copy-done.1
  13.2 0.0 copy-done.2
  13.2 0.0 copy-done.3
  13.2 1.4 %project.1 = (s32[16,33,1,128]{3,2,1,0:T(1,128)S(1)}, f32[64,128]{1,0:T(8,128)S(1)}, f32[64,128]{1,0:T(8,128)S(1)}) custom-call(s32[8,8]{1,0:T(8,128)S(1)} %bitcast.14, f32[136,128]{1,0:T(8,128)S(1)} %copy-done.2, f32[1024,128]{1,0:T(8,128)S(1)} %bitcast.12, bf16[1024,1024]{1,0:T(8,128)(2,1)S(1)} %bitcast.7, bf16[1024,128]{1,0:T(8,128)(2,1)S(1)} %bitcast.10), custom_call_target="tpu_custom_call" | custom-call | flops 67108864 | bytes 3289344 | tf_op jit(solution)/shard_map/project/pallas_call | solution.py:172
  14.6 32.8 %all_to_all.11.received = s32[16,33,1,128]{3,2,1,0:T(1,128)S(1)} all-to-all(s32[16,33,1,128]{3,2,1,0:T(1,128)S(1)} %get-tuple-element.7), channel_id=1, replica_groups={{0,32,64,96,128,160,192,224,256,288,320,352,384,416,448,480},{8,40,72,1..., dimensions={0} | all-to-all | bytes 540672 | tf_op jit(solution)/shard_map/all_to_all | solution.py:199
  47.3 1.4 %combine.1 = (s16[1032,128]{1,0:T(8,128)(2,1)S(1)}, f32[1024,128]{1,0:T(8,128)}) custom-call(f32[136,128]{1,0:T(8,128)S(1)} %copy-done.2, s32[16,33,1,128]{3,2,1,0:T(1,128)S(1)} %all_to_all.11.received, f32[64,128]{1,0:T(8,128)S(1)} %get-tuple-element.8.picked, f32[64,128]{1,0:T(8,128)S(1)} %get-tuple-element.9.left, f32[1024,128]{1,0:T(8,128)S(1)} %bitcast.13, ...), custom_call_target="tpu_custom_call" | custom-call | flops 268435456 | bytes 4077568 | tf_op jit(solution)/shard_map/combine/pallas_call | solution.py:172
  48.8 15.7 %all-gather.2 = s16[4128,128]{1,0:T(8,128)(2,1)S(1)} all-gather(s16[1032,128]{1,0:T(8,128)(2,1)S(1)} %get-tuple-element.11), channel_id=2, replica_groups={{0,8,16,24},{32,40,48,56},{64,72,80,88},{96,104,112,120},{128,136,144,1..., dimensions={0}, use_global_device_ids=true | all-gather | bytes 1320960 | tf_op jit(solution)/shard_map/all_gather | solution.py:209
  64.4 1.0 %finish.1 = f32[1024,128]{1,0:T(8,128)} custom-call(s16[4,1032,128]{2,1,0:T(8,128)(2,1)S(1)} %bitcast.9), custom_call_target="tpu_custom_call" | custom-call | bytes 1581056 | tf_op jit(solution)/shard_map/finish/pallas_call | solution.py:172
  (1 shorter events, 0.0 us)
Async XLA Ops:
  0.6 0.8 %copy-start.4 = (bf16[1,128,128]{2,1,0:T(8,128)(2,1)S(1)}, bf16[1,128,128]{2,1,0:T(8,128)(2,1)}, u32[]{:S(2)}) copy-start(bf16[1,128,128]{2,1,0:T(8,128)(2,1)} %param.7) | copy-start | bytes 98308
  1.4 11.8 %copy-start = (bf16[1,1024,1024]{2,1,0:T(8,128)(2,1)S(1)}, bf16[1,1024,1024]{2,1,0:T(8,128)(2,1)}, u32[]{:S(2)}) copy-start(bf16[1,1024,1024]{2,1,0:T(8,128)(2,1)} %param.6) | copy-start | bytes 6291460
  1.4 11.8 %copy-start.1 = (f32[1,1024,128]{2,1,0:T(8,128)S(1)}, f32[1,1024,128]{2,1,0:T(8,128)}, u32[]{:S(2)}) copy-start(f32[1,1024,128]{2,1,0:T(8,128)} %param.5) | copy-start | bytes 1572868
  1.4 11.8 %copy-start.2 = (f32[136,128]{1,0:T(8,128)S(1)}, f32[136,128]{1,0:T(8,128)}, u32[]{:S(2)}) copy-start(f32[136,128]{1,0:T(8,128)} %constant.2.clone.basis) | copy-start | bytes 208900
  1.4 11.8 %copy-start.3 = (s32[1,8,1,8]{3,2,1,0:T(1,128)S(1)}, s32[1,8,1,8]{3,2,1,0:T(1,128)}, u32[]{:S(2)}) copy-start(s32[1,8,1,8]{3,2,1,0:T(1,128)} %param.8) | copy-start | bytes 772

commit v7 on v6

--- a/solution.py
+++ b/solution.py
@@ -14,6 +14,7 @@
 PAIR = 2
 TOK = 1024
 NZ, NY = 16, 4
+EARLY = 32
 MOMENTUM_DECAY = 0.999
 AHEAD = 10**10
 BITS = 15
@@ -67,7 +68,24 @@
         copies[r, :, :] = out_grads[...]
 
 
-def project(chosen, basis, momentum, inputs, grads, message, picked, left):
+def subtract(picked, left, momentum, inputs, grads, new_momentum, moment, sems):
+    grad = dot(grads[...], inputs[...], ((0,), (0,)))
+    stores = []
+    for b in range(BLOCKS):
+        own_high, own_low = halves(picked[picks(b), :])
+        left_high, left_low = halves(left[picks(b), :])
+        own = jnp.concatenate([own_high, own_low, own_high], axis=0)
+        sent = dot(own, jnp.concatenate([left_high, left_high, left_low], axis=0), ((0,), (0,)))
+        moment[block(b), :] = MOMENTUM_DECAY * momentum[block(b), :] + grad[:, block(b)].T - sent
+        if b % PAIR == PAIR - 1:
+            done = slice((b + 1 - PAIR) * CH, (b + 1) * CH)
+            stores.append(pltpu.make_async_copy(moment.at[done, :], new_momentum.at[done, :], sems.at[b // PAIR]))
+            stores[-1].start()
+    for store in stores:
+        store.wait()
+
+
+def project(chosen, basis, momentum, inputs, grads, message, picked, left, new_momentum, moment, sems):
     wide = jnp.concatenate([chosen[...], jnp.zeros((BLOCKS, CH - K), I32)], axis=1)
     notes = jnp.sum(pltpu.roll(wide, 0, 1, stride=K, stride_axis=0), axis=0, keepdims=True)
     numbers = jnp.where(lax.broadcasted_iota(I32, (1, CH), 1) < PICKS, notes, CH)
@@ -105,20 +123,17 @@
             message[z, picks(i), 0, :] = word
         message[z, WORDS:, 0, :] = notes
 
-
-def combine(basis, received, picked, left, momentum, inputs, grads, message, new_momentum, moment, sems):
-    grad = dot(grads[...], inputs[...], ((0,), (0,)))
-    stores = []
-    for b in range(BLOCKS):
-        own_high, own_low = halves(picked[picks(b), :])
-        left_high, left_low = halves(left[picks(b), :])
-        own = jnp.concatenate([own_high, own_low, own_high], axis=0)
-        sent = dot(own, jnp.concatenate([left_high, left_high, left_low], axis=0), ((0,), (0,)))
-        moment[block(b), :] = MOMENTUM_DECAY * momentum[block(b), :] + grad[:, block(b)].T - sent
-        if b % PAIR == PAIR - 1:
-            done = slice((b + 1 - PAIR) * CH, (b + 1) * CH)
-            stores.append(pltpu.make_async_copy(moment.at[done, :], new_momentum.at[done, :], sems.at[b // PAIR]))
-            stores[-1].start()
+    @pl.when(lax.axis_index("rep") < EARLY)
+    def _():
+        subtract(picked, left, momentum, inputs, grads, new_momentum, moment, sems)
+
+
+def combine(basis, received, picked, left, momentum, inputs, grads, begun, message, new_momentum, moment, sems):
+    del begun
+    @pl.when(lax.axis_index("rep") >= EARLY)
+    def _():
+        subtract(picked, left, momentum, inputs, grads, new_momentum, moment, sems)
+
     notes = jnp.concatenate([received[:, WORDS, 0, :].astype(F32)] * K, axis=0).T
     own_slot = lax.broadcasted_iota(I32, (K, CH), 1) // NZ == lax.broadcasted_iota(I32, (K, CH), 0)
     notes = [jnp.sum(jnp.where(own_slot, notes[picks(i), :], 0.0), axis=0, keepdims=True) for i in range(2 * BLOCKS)]
@@ -147,8 +162,6 @@
             powers.append(power[:, i * CH : (i + 1) * CH])
             message[block(b + i), :] = coded[:, i * CH : (i + 1) * CH]
     message[BLOCKS * CH :, :] = jnp.concatenate(powers, axis=0).astype(I32).astype(I16)
-    for store in stores:
-        store.wait()
 
 
 def finish(received, update, total, sems):
@@ -165,7 +178,7 @@
         store.wait()
 
 
-def call(kernel, out, operands, spaces=None, flops=0, limit=4, scratch=(), results=None):
+def call(kernel, out, operands, spaces=None, flops=0, limit=4, scratch=(), results=None, aliases=None):
     spaces = spaces or [pltpu.VMEM] * len(operands)
     results = results or [pltpu.VMEM] * len(out)
     moved = sum(a.size * a.dtype.itemsize for a in operands) + sum(o.size * o.dtype.itemsize for o in out)
@@ -176,6 +189,7 @@
         in_specs=[pl.BlockSpec(memory_space=s) for s in spaces],
         out_specs=tuple(pl.BlockSpec(memory_space=s) for s in results),
         scratch_shapes=list(scratch),
+        input_output_aliases=aliases or {},
         compiler_params=pltpu.CompilerParams(vmem_limit_bytes=int(limit * 2**20)),
         cost_estimate=pl.CostEstimate(flops=flops, bytes_accessed=moved, transcendentals=0),
     )(*operands)
@@ -190,17 +204,22 @@
     table = jnp.asarray(basis_rows())
     (copies,) = call(spread, [array((ROWS,) + out_grads.shape[1:], BF16)], [out_grads[0]], flops=AHEAD)
     grads = lax.all_to_all(copies, "row", 0, 0, tiled=True).reshape(TOK, CH)
-    message, picked, left = call(
+    message, picked, left, new_momentum = call(
         project,
-        [array((NZ, WORDS + 1, 1, CH), I32), array((PICKS, CH)), array((PICKS, CH))],
+        [array((NZ, WORDS + 1, 1, CH), I32), array((PICKS, CH)), array((PICKS, CH)), array((BLOCKS * CH, CH))],
         [chosen.reshape(BLOCKS, K), table, momentum, inputs, grads],
         flops=2 * 2 * 2 * PICKS * CH * TOK,
+        limit=8,
+        scratch=[pltpu.VMEM((BLOCKS * CH, CH), F32), pltpu.SemaphoreType.DMA((BLOCKS // PAIR,))],
+        results=[pltpu.VMEM, pltpu.VMEM, pltpu.VMEM, pl.ANY],
     )
     along_z = lax.all_to_all(message, "rep", 0, 0, axis_index_groups=Z_GROUPS, tiled=True)
     message, new_momentum = call(
         combine,
         [array((BLOCKS * CH + BLOCKS, CH), I16), array((BLOCKS * CH, CH))],
-        [table, along_z, picked, left, momentum, inputs, grads],
+        [table, along_z, picked, left, momentum, inputs, grads, new_momentum],
+        spaces=[pltpu.VMEM] * 7 + [pl.ANY],
+        aliases={7: 1},
         limit=8,
         flops=2 * BLOCKS * CH * CH * TOK,
         scratch=[pltpu.VMEM((BLOCKS * CH, CH), F32), pltpu.SemaphoreType.DMA((BLOCKS // PAIR,))],

time: 65.6 us -> 65.2 us (level)
  blocking collectives: 60.2 us -> 58.9 us
  Pallas kernels: 3.76 us -> 4.68 us
    all_to_all x1, blocking collectives: 32.8 us -> 31.5 us  [body(): lax.all_to_all(message, 'rep', 0, 0, axis_index_groups=Z_GROUPS, tiled=True)]
    pallas_call x4, Pallas kernels: 3.76 us -> 4.68 us  [call(): pl.pallas_call(kernel, name=kernel.__name__, out_shape=tuple(out), in_spe...]
where the time goes in v7:
time: 65.2 us; the launch traced here: 65 us
  blocking collectives  58.9 us (90%)
  Pallas kernels  4.68 us (7%)
  local copies, waits for them, and re-layouts  0.77 us (1%)
  between operations  0.68 us (1%)
    all_to_all x1, blocking collectives, body(): lax.all_to_all(message, 'rep', 0, 0, axis_index_groups=Z_GROUPS, tiled=True)  31.5 us
    all_gather x1, blocking collectives, body(): along_y = lax.all_gather(message, 'rep', axis_index_groups=Y_GROUPS)  15.6 us
    all_to_all x1, blocking collectives, body(): grads = lax.all_to_all(copies, 'row', 0, 0, tiled=True).reshape(TOK, CH)  11.7 us
    pallas_call x4, Pallas kernels, call(): pl.pallas_call(kernel, name=kernel.__name__, out_shape=tuple(out), in_spe...  4.68 us

profile of v7, /device:TPU:64, one launch (start us, length us, event | category | flops | bytes accessed | tf_op | source)
XLA Modules:
  0.0 65.0 jit_solution(15384102513274182425)
XLA Ops:
  0.6 0.0 copy-start.4
  0.6 0.7 %copy-done.4 = bf16[1,128,128]{2,1,0:T(8,128)(2,1)S(1)} copy-done((bf16[1,128,128]{2,1,0:T(8,128)(2,1)S(1)}, bf16[1,128,128]{2,1,0:T(8,128)(2,1)}, u32[]{:S(2)}) %copy-start.4) | copy-done | bytes 32792
  1.4 0.0 copy-start
  1.4 0.0 copy-start.1
  1.4 0.0 copy-start.2
  1.4 0.0 copy-start.3
  1.4 11.7 %all_to_all.10 = bf16[8,128,128]{2,1,0:T(8,128)(2,1)S(1)} all-to-all(bf16[8,128,128]{2,1,0:T(8,128)(2,1)S(1)} %spread.1), channel_id=1, replica_groups=mesh['rep'=64,'row'=8] {'row'}, dimensions={0} | all-to-all | bytes 524288 | tf_op jit(solution)/shard_map/all_to_all | solution.py:206
  13.2 0.0 copy-done
  13.2 0.0 copy-done.1
  13.2 0.0 copy-done.2
  13.2 0.0 copy-done.3
  13.2 2.7 %project.1 = (s32[16,33,1,128]{3,2,1,0:T(1,128)S(1)}, f32[64,128]{1,0:T(8,128)S(1)}, f32[64,128]{1,0:T(8,128)S(1)}, f32[1024,128]{1,0:T(8,128)}) custom-call(s32[8,8]{1,0:T(8,128)S(1)} %bitcast.14, f32[136,128]{1,0:T(8,128)S(1)} %copy-done.2, f32[1024,128]{1,0:T(8,128)S(1)} %bitcast.12, bf16[1024,1024]{1,0:T(8,128)(2,1)S(1)} %bitcast.7, ...), custom_call_target="tpu_custom_call" | custom-call | flops 67108864 | bytes 3813632 | tf_op jit(solution)/shard_map/project/pallas_call | solution.py:185
  15.9 31.5 %all_to_all.11.received = s32[16,33,1,128]{3,2,1,0:T(1,128)S(1)} all-to-all(s32[16,33,1,128]{3,2,1,0:T(1,128)S(1)} %get-tuple-element.8), channel_id=1, replica_groups={{0,32,64,96,128,160,192,224,256,288,320,352,384,416,448,480},{8,40,72,1..., dimensions={0} | all-to-all | bytes 540672 | tf_op jit(solution)/shard_map/all_to_all | solution.py:216
  47.4 1.0 %combine.1 = (s16[1032,128]{1,0:T(8,128)(2,1)S(1)}, f32[1024,128]{1,0:T(8,128)}) custom-call(f32[136,128]{1,0:T(8,128)S(1)} %copy-done.2, s32[16,33,1,128]{3,2,1,0:T(1,128)S(1)} %all_to_all.11.received, f32[64,128]{1,0:T(8,128)S(1)} %get-tuple-element.9.picked, f32[64,128]{1,0:T(8,128)S(1)} %get-tuple-element.10.left, ...), custom_call_target="tpu_custom_call", output_to_operand_aliasing={{1}: (7, {})} | custom-call | flops 268435456 | bytes 4601856 | tf_op jit(solution)/shard_map/combine/pallas_call | solution.py:185
  48.4 15.6 %all-gather.2 = s16[4128,128]{1,0:T(8,128)(2,1)S(1)} all-gather(s16[1032,128]{1,0:T(8,128)(2,1)S(1)} %get-tuple-element.13), channel_id=2, replica_groups={{0,8,16,24},{32,40,48,56},{64,72,80,88},{96,104,112,120},{128,136,144,1..., dimensions={0}, use_global_device_ids=true | all-gather | bytes 1320960 | tf_op jit(solution)/shard_map/all_gather | solution.py:228
  64.0 1.0 %finish.1 = f32[1024,128]{1,0:T(8,128)} custom-call(s16[4,1032,128]{2,1,0:T(8,128)(2,1)S(1)} %bitcast.9), custom_call_target="tpu_custom_call" | custom-call | bytes 1581056 | tf_op jit(solution)/shard_map/finish/pallas_call | solution.py:185
  (1 shorter events, 0.0 us)
Async XLA Ops:
  0.6 0.8 %copy-start.4 = (bf16[1,128,128]{2,1,0:T(8,128)(2,1)S(1)}, bf16[1,128,128]{2,1,0:T(8,128)(2,1)}, u32[]{:S(2)}) copy-start(bf16[1,128,128]{2,1,0:T(8,128)(2,1)} %param.7) | copy-start | bytes 98308
  1.4 11.8 %copy-start = (bf16[1,1024,1024]{2,1,0:T(8,128)(2,1)S(1)}, bf16[1,1024,1024]{2,1,0:T(8,128)(2,1)}, u32[]{:S(2)}) copy-start(bf16[1,1024,1024]{2,1,0:T(8,128)(2,1)} %param.6) | copy-start | bytes 6291460
  1.4 11.8 %copy-start.1 = (f32[1,1024,128]{2,1,0:T(8,128)S(1)}, f32[1,1024,128]{2,1,0:T(8,128)}, u32[]{:S(2)}) copy-start(f32[1,1024,128]{2,1,0:T(8,128)} %param.5) | copy-start | bytes 1572868
  1.4 11.8 %copy-start.2 = (f32[136,128]{1,0:T(8,128)S(1)}, f32[136,128]{1,0:T(8,128)}, u32[]{:S(2)}) copy-start(f32[136,128]{1,0:T(8,128)} %constant.2.clone.basis) | copy-start | bytes 208900
  1.4 11.8 %copy-start.3 = (s32[1,8,1,8]{3,2,1,0:T(1,128)S(1)}, s32[1,8,1,8]{3,2,1,0:T(1,128)}, u32[]{:S(2)}) copy-start(s32[1,8,1,8]{3,2,1,0:T(1,128)} %param.8) | copy-start | bytes 772

commit v8 on v7

--- a/solution.py
+++ b/solution.py
@@ -11,7 +11,7 @@
 BLOCKS = 8
 PICKS = BLOCKS * K
 ROWS = 8
-PAIR = 2
+PAIR = 1
 TOK = 1024
 NZ, NY = 16, 4
 EARLY = 32

time: 65.2 us -> 65.3 us (level)
  the two profiles are of different devices: /device:TPU:64 before, /device:TPU:40 now
where the time goes in v8:
time: 65.3 us; the launch traced here: 65.1 us
  blocking collectives  58.9 us (90%)
  Pallas kernels  4.76 us (7%)
  local copies, waits for them, and re-layouts  0.77 us (1%)
  between operations  0.68 us (1%)
    all_to_all x1, blocking collectives, body(): lax.all_to_all(message, 'rep', 0, 0, axis_index_groups=Z_GROUPS, tiled=True)  31.6 us
    all_gather x1, blocking collectives, body(): along_y = lax.all_gather(message, 'rep', axis_index_groups=Y_GROUPS)  15.5 us
    all_to_all x1, blocking collectives, body(): grads = lax.all_to_all(copies, 'row', 0, 0, tiled=True).reshape(TOK, CH)  11.7 us
    pallas_call x4, Pallas kernels, call(): pl.pallas_call(kernel, name=kernel.__name__, out_shape=tuple(out), in_spe...  4.76 us

profile of v8, /device:TPU:40, one launch (start us, length us, event | category | flops | bytes accessed | tf_op | source)
XLA Modules:
  0.0 65.1 jit_solution(18311423707154728529)
XLA Ops:
  0.6 0.0 copy-start.4
  0.6 0.7 %copy-done.4 = bf16[1,128,128]{2,1,0:T(8,128)(2,1)S(1)} copy-done((bf16[1,128,128]{2,1,0:T(8,128)(2,1)S(1)}, bf16[1,128,128]{2,1,0:T(8,128)(2,1)}, u32[]{:S(2)}) %copy-start.4) | copy-done | bytes 32792
  1.4 0.0 copy-start
  1.4 0.0 copy-start.1
  1.4 0.0 copy-start.2
  1.4 0.0 copy-start.3
  1.4 11.7 %all_to_all.10 = bf16[8,128,128]{2,1,0:T(8,128)(2,1)S(1)} all-to-all(bf16[8,128,128]{2,1,0:T(8,128)(2,1)S(1)} %spread.1), channel_id=1, replica_groups=mesh['rep'=64,'row'=8] {'row'}, dimensions={0} | all-to-all | bytes 524288 | tf_op jit(solution)/shard_map/all_to_all | solution.py:206
  13.2 0.0 copy-done
  13.2 0.0 copy-done.1
  13.2 0.0 copy-done.2
  13.2 0.0 copy-done.3
  13.2 2.7 %project.1 = (s32[16,33,1,128]{3,2,1,0:T(1,128)S(1)}, f32[64,128]{1,0:T(8,128)S(1)}, f32[64,128]{1,0:T(8,128)S(1)}, f32[1024,128]{1,0:T(8,128)}) custom-call(s32[8,8]{1,0:T(8,128)S(1)} %bitcast.14, f32[136,128]{1,0:T(8,128)S(1)} %copy-done.2, f32[1024,128]{1,0:T(8,128)S(1)} %bitcast.12, bf16[1024,1024]{1,0:T(8,128)(2,1)S(1)} %bitcast.7, ...), custom_call_target="tpu_custom_call" | custom-call | flops 67108864 | bytes 3813632 | tf_op jit(solution)/shard_map/project/pallas_call | solution.py:185
  15.9 31.6 %all_to_all.11.received = s32[16,33,1,128]{3,2,1,0:T(1,128)S(1)} all-to-all(s32[16,33,1,128]{3,2,1,0:T(1,128)S(1)} %get-tuple-element.8), channel_id=1, replica_groups={{0,32,64,96,128,160,192,224,256,288,320,352,384,416,448,480},{8,40,72,1..., dimensions={0} | all-to-all | bytes 540672 | tf_op jit(solution)/shard_map/all_to_all | solution.py:216
  47.6 1.0 %combine.1 = (s16[1032,128]{1,0:T(8,128)(2,1)S(1)}, f32[1024,128]{1,0:T(8,128)}) custom-call(f32[136,128]{1,0:T(8,128)S(1)} %copy-done.2, s32[16,33,1,128]{3,2,1,0:T(1,128)S(1)} %all_to_all.11.received, f32[64,128]{1,0:T(8,128)S(1)} %get-tuple-element.9.picked, f32[64,128]{1,0:T(8,128)S(1)} %get-tuple-element.10.left, ...), custom_call_target="tpu_custom_call", output_to_operand_aliasing={{1}: (7, {})} | custom-call | flops 268435456 | bytes 4601856 | tf_op jit(solution)/shard_map/combine/pallas_call | solution.py:185
  48.6 15.5 %all-gather.2 = s16[4128,128]{1,0:T(8,128)(2,1)S(1)} all-gather(s16[1032,128]{1,0:T(8,128)(2,1)S(1)} %get-tuple-element.13), channel_id=2, replica_groups={{0,8,16,24},{32,40,48,56},{64,72,80,88},{96,104,112,120},{128,136,144,1..., dimensions={0}, use_global_device_ids=true | all-gather | bytes 1320960 | tf_op jit(solution)/shard_map/all_gather | solution.py:228
  64.1 1.0 %finish.1 = f32[1024,128]{1,0:T(8,128)} custom-call(s16[4,1032,128]{2,1,0:T(8,128)(2,1)S(1)} %bitcast.9), custom_call_target="tpu_custom_call" | custom-call | bytes 1581056 | tf_op jit(solution)/shard_map/finish/pallas_call | solution.py:185
  (1 shorter events, 0.0 us)
Async XLA Ops:
  0.6 0.8 %copy-start.4 = (bf16[1,128,128]{2,1,0:T(8,128)(2,1)S(1)}, bf16[1,128,128]{2,1,0:T(8,128)(2,1)}, u32[]{:S(2)}) copy-start(bf16[1,128,128]{2,1,0:T(8,128)(2,1)} %param.7) | copy-start | bytes 98308
  1.4 11.8 %copy-start = (bf16[1,1024,1024]{2,1,0:T(8,128)(2,1)S(1)}, bf16[1,1024,1024]{2,1,0:T(8,128)(2,1)}, u32[]{:S(2)}) copy-start(bf16[1,1024,1024]{2,1,0:T(8,128)(2,1)} %param.6) | copy-start | bytes 6291460
  1.4 11.8 %copy-start.1 = (f32[1,1024,128]{2,1,0:T(8,128)S(1)}, f32[1,1024,128]{2,1,0:T(8,128)}, u32[]{:S(2)}) copy-start(f32[1,1024,128]{2,1,0:T(8,128)} %param.5) | copy-start | bytes 1572868
  1.4 11.8 %copy-start.2 = (f32[136,128]{1,0:T(8,128)S(1)}, f32[136,128]{1,0:T(8,128)}, u32[]{:S(2)}) copy-start(f32[136,128]{1,0:T(8,128)} %constant.2.clone.basis) | copy-start | bytes 208900
  1.4 11.8 %copy-start.3 = (s32[1,8,1,8]{3,2,1,0:T(1,128)S(1)}, s32[1,8,1,8]{3,2,1,0:T(1,128)}, u32[]{:S(2)}) copy-start(s32[1,8,1,8]{3,2,1,0:T(1,128)} %param.8) | copy-start | bytes 772
